TPU v7x, 256 devices: a whole 4x4x8 slice. The times are simulated.
256 devices in a mesh: dp: 128 (over z, y, x), col: 2 (over core).
Axes of the slice: x: 4, y: 4, z: 8, core: 2. Of those that a mesh axis runs over, the one named last changes fastest.
Arguments:
- item_owner: int32 [131072, 1], P('dp'), may hold values from 0 to 127; in each aligned block of 1024 rows (0 to 1023, 1024 to 2047, ...) at most 10 rows name the same one
- item_row: int32 [131072], P('dp'), may hold values from 0 to 4095
- seq_lengths: int32 [128, 8], P('dp'), may hold values from 1 to 256, 1024 in all within a row
- table: bfloat16 [524288, 1024], P('dp', 'col'), may hold values from -6 to 6
- w_qkvu: bfloat16 [1024, 4096], P(None, 'col'), may hold values from -0.1875 to 0.1875
- w_out: bfloat16 [1024, 1024], P('col'), may hold values from -0.1875 to 0.1875
Outputs:
- layer_out: bfloat16 [131072, 1024], P('dp', 'col')
Inputs may be any that keep to these rules, and one draw needn't show every extreme that they name: `item_owner`: the tokens of one data group name one table shard at most 10 times; in every draw some data group names some shard exactly 10 times. `seq_lengths`: each row sums to 1024; its largest entry is exactly 256.
All inputs are finite; a program needn't handle non-finite values.
Results may differ from a plain program's by a relative error of at most 0.0065.
Values may be sent and summed in bfloat16 or wider, within the bound.
No kernel may reach another device: no remote copies, remote signals or barrier semaphores. Data moves between devices by JAX's collectives and lax.ppermute only.
A program may use at most 64 MiB of HBM per device.

v0:
```python
import jax
import jax.numpy as jnp
from jax import lax
from jax.sharding import PartitionSpec as P

D = 1024
DH = 128
MAX_LEN = 256


def from_everyone(x, axis):
    size = lax.axis_size(axis)
    return lax.all_to_all(jnp.broadcast_to(x[None], (size, *x.shape)), axis, 0, 0, tiled=True)


def joined_along(tiles, dim):
    shape = list(tiles.shape[1:])
    shape[dim] *= tiles.shape[0]
    return jnp.moveaxis(tiles, 0, dim).reshape(shape)


def gathered_copies(x, axis, dim):
    tiles = from_everyone(x, axis)
    return joined_along(tiles, dim)


def over_copies(x, axis):
    everything = from_everyone(x, axis)
    return jnp.sum(everything, axis=0)


def together(arrays, axis):
    ends = [0]
    for a in arrays:
        ends.append(ends[-1] + a.size)
    subtotal = over_copies(jnp.concatenate([a.ravel() for a in arrays]), axis)
    return tuple((subtotal[b:e].reshape(a.shape) for a, b, e in zip(arrays, ends, ends[1:])))


def local(item_owner, item_row, seq_lengths, table, w_qkvu, w_out):
    tokens = item_row.shape[0]
    peers = lax.axis_size("dp")
    slots = tokens // peers + max(1, tokens // (4 * peers))
    owner = item_owner[:, 0]
    onehot = (owner[:, None] == jnp.arange(peers, dtype=jnp.int32)[None, :]).astype(jnp.int32)
    running = jnp.cumsum(onehot, axis=0) - 1
    slot = jnp.sum(onehot * running, axis=1)
    wanted = jnp.zeros((peers, slots), jnp.int32).at[owner, slot].set(item_row)
    fetched = jnp.take(
        table, lax.all_to_all(wanted, "dp", split_axis=0, concat_axis=0, tiled=True), axis=0
    )
    arrived = lax.all_to_all(fetched, "dp", split_axis=0, concat_axis=0, tiled=True)
    emb = arrived[owner, slot]
    width = w_qkvu.shape[1]
    rows_w = w_qkvu
    proj = jnp.dot(gathered_copies(emb, "col", 1), rows_w, preferred_element_type=jnp.float32)
    local_heads = width // (4 * DH)
    qkvu = jax.nn.silu(proj).astype(jnp.bfloat16).reshape(tokens, local_heads, 4, DH)
    query = qkvu[:, :, 0, :]
    keys = qkvu[:, :, 1, :]
    values = qkvu[:, :, 2, :]
    gates = qkvu[:, :, 3, :].reshape(tokens, local_heads * DH)
    ends = jnp.cumsum(seq_lengths[0])
    position = jnp.arange(tokens)
    segment = jnp.sum((ends[None, :] <= position[:, None]).astype(jnp.int32), axis=1)
    visible = (segment[:, None] == segment[None, :]) & (position[None, :] <= position[:, None])
    scores = jnp.einsum("qhd,khd->hqk", query, keys, preferred_element_type=jnp.float32) / jnp.sqrt(
        jnp.float32(DH)
    )
    weights = (jnp.where(visible[None], jax.nn.silu(scores), 0.0) / MAX_LEN).astype(jnp.bfloat16)
    attn = jnp.einsum("hqk,khd->qhd", weights, values, preferred_element_type=jnp.float32).reshape(
        tokens, local_heads * DH
    )
    totals, squares = together((jnp.sum(attn, axis=1), jnp.sum(attn * attn, axis=1)), "col")
    mean = (totals / D)[:, None]
    msq = (squares / D)[:, None]
    normed = (attn - mean) / jnp.sqrt(msq - mean * mean + 1e-05)
    hidden = (normed * gates.astype(jnp.float32)).astype(jnp.bfloat16)
    out_slice = lax.all_to_all(w_out, "col", split_axis=1, concat_axis=0, tiled=True)
    rows_w = out_slice
    mixed = jnp.dot(gathered_copies(hidden, "col", 1), rows_w, preferred_element_type=jnp.float32)
    return (emb.astype(jnp.float32) + mixed).astype(jnp.bfloat16)


def solution(mesh):
    return jax.shard_map(
        local,
        mesh=mesh,
        in_specs=(
            P("dp", None),
            P("dp"),
            P("dp", None),
            P("dp", "col"),
            P(None, "col"),
            P("col", None),
        ),
        out_specs=P("dp", "col"),
        check_vma=False,
    )
```

profile of v0, /device:TPU:1, one launch (start us, length us, event | category | flops | bytes accessed | tf_op | source)
XLA Modules:
  0.0 187.1 jit_solution(11151644055285792051)
XLA Ops:
  0.0 0.9 copy.62
  1.9 4.5 %scatter_custom_fusion = s32[1280]{0:T(1024)S(1)} fusion(s32[1024]{0:T(1024)S(1)} %broadcast_select_fusion.1, s32[1024]{0:T(1024)} %param.7, s32[]{:T(128)} %constant.25.clone.1), kind=kCustom, calls=%fused_computation.51 | custom fusion | bytes 5632
  6.5 26.9 %all_to_all.52 = s32[128,1,10]{2,1,0:T(1,128)S(1)} all-to-all(s32[128,1,10]{2,1,0:T(1,128)S(1)} %copy.64), channel_id=1, replica_groups=mesh['dp'=128,'col'=2] {'dp'}, dimensions={0} | all-to-all | bytes 10240 | tf_op jit(solution)/shard_map/all_to_all | solution.py:50
  33.5 6.9 %gather_fusion = bf16[1280,512]{1,0:T(8,128)(2,1)S(1)} fusion(bf16[4096,512]{1,0:T(8,128)(2,1)} %param.9, s32[2048]{0:T(1024)S(1)} %pad_clamp_fusion), kind=kCustom, calls=%fused_computation | custom fusion | bytes 2626560 | tf_op jit(solution)/shard_map/jit(_take)/gather | solution.py:49
  40.9 1.6 broadcast_select_fusion
  42.5 6.3 %all-to-all-start.1 = ((bf16[128,10,512]{2,1,0:T(8,128)(2,1)}), bf16[128,10,512]{2,1,0:T(8,128)(2,1)S(1)}, u32[]{:S(2)}, u32[]{:S(2)}) async-start(bf16[128,10,512]{2,1,0:T(8,128)(2,1)} %broadcast_select_fusion), calls=%async_computation.1 | async-start | bytes 4194304 | tf_op jit(solution)/shard_map/all_to_all | solution.py:52
  49.0 1.5 copy.73
  50.5 1.3 copy.74
  52.0 1.6 fusion
  53.5 43.8 %all-to-all-done.1 = bf16[128,10,512]{2,1,0:T(8,128)(2,1)S(1)} async-done(((bf16[128,10,512]{2,1,0:T(8,128)(2,1)}), bf16[128,10,512]{2,1,0:T(8,128)(2,1)S(1)}, u32[]{:S(2)}, u32[]{:S(2)}) %all-to-all-start.1) | async-done | bytes 1310752 | tf_op jit(solution)/shard_map/all_to_all | solution.py:52
  97.3 0.7 copy.65
  98.0 7.2 %gather_fusion.1 = bf16[1024,512]{1,0:T(8,128)(2,1)S(1)} fusion(bf16[128,10,512]{2,0,1:T(8,128)(2,1)S(1)} %copy.65, s32[1024]{0:T(1024)S(1)} %bitcast.73), kind=kCustom, calls=%fused_computation.1 | custom fusion | bytes 2105344 | tf_op jit(solution)/shard_map/gather | solution.py:53
  106.2 10.6 %all_to_all.53 = bf16[2,1024,512]{1,2,0:T(8,128)(2,1)S(1)} all-to-all(bf16[2,1024,512]{1,2,0:T(8,128)(2,1)S(1)} %broadcast_in_dim.36), channel_id=1, replica_groups=mesh['dp'=128,'col'=2] {'col'}, dimensions={0} | all-to-all | bytes 4194304 | tf_op jit(solution)/shard_map/all_to_all | solution.py:13
  116.8 7.6 %multiply_convert_fusion.1 = bf16[1024,2048]{1,0:T(8,128)(2,1)} fusion(bf16[1024,1024]{0,1:T(8,128)(2,1)S(1)} %bitcast.75, bf16[1024,2048]{1,0:T(8,128)(2,1)S(1)} %copy-done.5), kind=kOutput, calls=%fused_computation.4 | convolution fusion | flops 4305453056 | bytes 10485760 | tf_op jit(solution)/shard_map/dot_general | solution.py:56
  124.3 7.7 %reshape.194 = bf16[1024,4,4,128]{3,2,1,0:T(4,128)(2,1)} reshape(bf16[1024,2048]{1,0:T(8,128)(2,1)} %multiply_convert_fusion.1) | data formatting | bytes 8388608 | tf_op jit(solution)/shard_map/reshape | solution.py:58
  132.0 14.7 %slice_convert_fusion = (f32[1024,4,1,128]{3,2,1,0:T(1,128)}, bf16[1024,4,1,128]{3,2,1,0:T(2,128)(2,1)S(1)}, bf16[1024,4,1,128]{3,2,1,0:T(2,128)(2,1)}, bf16[1024,4,1,128]{3,2,1,0:T(2,128)(2,1)}) fusion(bf16[1024,4,4,128]{3,2,1,0:T(4,128)(2,1)} %reshape.194), kind=kLoop, calls=%fused_computation.8 | loop fusion | flops 524288 | bytes 9437184 | tf_op jit(solution)/shard_map/convert_element_type | solution.py:78
  146.7 2.6 %copy.77 = bf16[1024,4,1,128]{0,3,1,2:T(8,128)(2,1)S(1)} copy(bf16[1024,4,1,128]{3,2,1,0:T(2,128)(2,1)S(1)} %get-tuple-element.6) | data formatting | bytes 2097152
  149.4 11.6 %fusion.8 = (f32[1024]{0:T(1024)S(1)}, f32[4,128,1024]{2,1,0:T(8,128)S(1)}) fusion(pred[1024,1024]{1,0:T(8,128)(4,1)} %fusion, bf16[1024,4,1,128]{3,2,1,0:T(2,128)(2,1)} %get-tuple-element.7, bf16[1024,4,1,128]{3,2,1,0:T(2,128)(2,1)} %get-tuple-element.8, bf16[1024,4,1,128]{0,3,1,2:T(8,128)(2,1)S(1)} %copy.77), kind=kOutput, calls=%fused_computation.18 | convolution fusion | flops 2182085632 | bytes 6295552 | tf_op jit(solution)/shard_map/hqk,khd->qhd/dot_general | solution.py:71
  161.1 3.7 %all_to_all.54 = f32[2,1,2048]{2,1,0:T(1,128)S(1)} all-to-all(f32[2,1,2048]{2,1,0:T(1,128)S(1)} %broadcast_in_dim.39), channel_id=1, replica_groups=mesh['dp'=128,'col'=2] {'col'}, dimensions={0} | all-to-all | bytes 32768 | tf_op jit(solution)/shard_map/all_to_all | solution.py:13
  164.8 4.7 %all-to-all-start.5 = ((bf16[512,2,512]{2,0,1:T(8,128)(2,1)}), bf16[512,2,512]{2,0,1:T(8,128)(2,1)}, u32[]{:S(2)}, u32[]{:S(2)}) async-start(bf16[512,2,512]{2,0,1:T(8,128)(2,1)} %copy.74), calls=%async_computation.5 | async-start | bytes 2097152 | tf_op jit(solution)/shard_map/all_to_all | solution.py:79
  169.6 6.1 %copy.75 = f32[1024,4,1,128]{0,3,1,2:T(8,128)} copy(f32[1024,4,1,128]{3,2,1,0:T(1,128)} %get-tuple-element.5) | data formatting | bytes 4194304 | tf_op jit(solution)/shard_map/convert_element_type | solution.py:78
  175.7 2.1 %fusion.4 = bf16[1024,512]{0,1:T(8,128)(2,1)S(1)} fusion(f32[4,128,1024]{2,1,0:T(8,128)S(1)} %get-tuple-element.15, f32[1024,4,1,128]{0,3,1,2:T(8,128)} %copy.75, f32[1024]{0:T(1024)S(1)} %get-tuple-element.10, f32[1024]{0:T(1024)S(1)} %get-tuple-element.9), kind=kLoop, calls=%fused_computation.12 | loop fusion | flops 2097152 | bytes 5251072 | tf_op jit(solution)/shard_map/convert_element_type | solution.py:78
  178.5 5.2 %all_to_all.55 = bf16[2,1024,512]{2,1,0:T(8,128)(2,1)S(1)} all-to-all(bf16[2,1024,512]{2,1,0:T(8,128)(2,1)S(1)} %broadcast_in_dim.40), channel_id=1, replica_groups=mesh['dp'=128,'col'=2] {'col'}, dimensions={0} | all-to-all | bytes 4194304 | tf_op jit(solution)/shard_map/all_to_all | solution.py:13
  183.7 3.4 %fusion.5 = bf16[1024,512]{1,0:T(8,128)(2,1)} fusion(bf16[1024,512]{1,0:T(8,128)(2,1)S(1)} %copy-done.1, bf16[2,1024,512]{2,1,0:T(8,128)(2,1)S(1)} %all_to_all.55, bf16[512,2,512]{2,0,1:T(8,128)(2,1)} %all-to-all-done.5), kind=kOutput, calls=%fused_computation.14 | convolution fusion | flops 1075314688 | bytes 5242880 | tf_op jit(solution)/shard_map/dot_general | solution.py:81
  (43 shorter events, 3.8 us)
Async XLA Ops:
  0.0 1.7 copy-start.4
  0.0 1.8 copy-start.3
  0.0 1.3 copy-start.2
  42.5 6.4 %copy-start.6 = (s32[1,8]{1,0:T(1,128)S(1)}, s32[1,8]{1,0:T(1,128)}, u32[]{:S(2)}) copy-start(s32[1,8]{1,0:T(1,128)} %param.8) | copy-start | bytes 100
  42.5 54.8 %all-to-all-start.1 = ((bf16[128,10,512]{2,1,0:T(8,128)(2,1)}), bf16[128,10,512]{2,1,0:T(8,128)(2,1)S(1)}, u32[]{:S(2)}, u32[]{:S(2)}) async-start(bf16[128,10,512]{2,1,0:T(8,128)(2,1)} %broadcast_select_fusion), calls=%async_computation.1 | async-start | bytes 4194304 | tf_op jit(solution)/shard_map/all_to_all | solution.py:52
  105.2 1.0 copy-start
  106.2 10.6 %copy-start.5 = (bf16[1024,2048]{1,0:T(8,128)(2,1)S(1)}, bf16[1024,2048]{1,0:T(8,128)(2,1)}, u32[]{:S(2)}) copy-start(bf16[1024,2048]{1,0:T(8,128)(2,1)} %param.10) | copy-start | bytes 12582916
  164.8 13.5 %all-to-all-start.5 = ((bf16[512,2,512]{2,0,1:T(8,128)(2,1)}), bf16[512,2,512]{2,0,1:T(8,128)(2,1)}, u32[]{:S(2)}, u32[]{:S(2)}) async-start(bf16[512,2,512]{2,0,1:T(8,128)(2,1)} %copy.74), calls=%async_computation.5 | async-start | bytes 2097152 | tf_op jit(solution)/shard_map/all_to_all | solution.py:79
  178.5 5.2 %copy-start.1 = (bf16[1024,512]{1,0:T(8,128)(2,1)S(1)}, bf16[1024,512]{1,0:T(8,128)(2,1)}, u32[]{:S(2)}) copy-start(bf16[1024,512]{1,0:T(8,128)(2,1)} %copy-done) | copy-start | bytes 3145732
where the time goes:
time: 188 us; the launch traced here: 187 us
  blocking collectives  46.4 us (25%)
  waiting for transfers between devices  43.8 us (23%)
  local copies, waits for them, and re-layouts  41.8 us (22%)
  matrix products  22.6 us (12%)
  other arithmetic  21.3 us (11%)
  starting transfers between devices  11.1 us (6%)
    all_to_all x1, waiting for transfers between devices, local(): lax.all_to_all(fetched, 'dp', split_axis=0, concat_axis=0, tiled=True)  43.8 us
    all_to_all x1, blocking collectives, local(): lax.all_to_all(wanted, 'dp', split_axis=0, concat_axis=0, tiled=True)  26.9 us
    all_to_all x3, blocking collectives, from_everyone(): lax.all_to_all(jnp.broadcast_to(x[None], (size, *x.shape)), axis, 0, 0, t...  19.5 us
    convert_element_type x2, other arithmetic, local(): hidden = (normed * gates.astype(jnp.float32)).astype(jnp.bfloat16)  16.8 us
    dot_general x1, matrix products, local(): jnp.einsum('hqk,khd->qhd', weights, values, preferred_element_type=jnp.fl...  11.6 us
    unnamed x17, local copies, waits for them, and re-layouts  8.67 us
    gather x2, local copies, waits for them, and re-layouts, local(): emb = arrived[owner, slot]  7.72 us
    reshape x1, local copies, waits for them, and re-layouts, local(): jax.nn.silu(proj).astype(jnp.bfloat16).reshape(tokens, local_heads, 4, DH)  7.7 us
  transfers between devices with their start and end apart: 2, of which 1 were waited for; matrix products, arithmetic and copies ran while one was open for 7% of the time, Pallas kernels for 0%

commit v1 on v0

v1 whole, which is shorter than its diff:
```python
import jax
import jax.numpy as jnp
from jax import lax
from jax.experimental import pallas as pl
from jax.experimental.pallas import tpu as pltpu
from jax.sharding import PartitionSpec as P

D = 1024
DH = 128
MAX_LEN = 256
TOK = 1024
HALF = 512
CAP = 10
WIN = HALF + MAX_LEN
LOCAL = 4
F32 = jnp.float32
BF16 = jnp.bfloat16
NT = (((1,), (1,)), ((), ()))


def route_kernel(owner_ref, row_ref, wanted_ref, dest_ref):
    sub = lax.broadcasted_iota(jnp.int32, (128, 128), 0)
    lane = lax.broadcasted_iota(jnp.int32, (128, 128), 1)
    before = (sub < lane).astype(F32).astype(BF16)
    count = jnp.zeros((128, 1), F32)
    high = jnp.zeros((128, 128), F32)
    low = jnp.zeros((128, 128), F32)
    for b in range(TOK // 128):
        owner = owner_ref[b : b + 1, :]
        row = row_ref[b : b + 1, :]
        hit = (sub == owner).astype(F32)
        hit16 = hit.astype(BF16)
        rank = jnp.dot(hit16, before, preferred_element_type=F32) + count
        slot = jnp.sum(hit * rank, axis=0, keepdims=True).astype(jnp.int32)
        count = count + jnp.sum(hit, axis=1, keepdims=True)
        dest_ref[b : b + 1, :] = owner * CAP + slot
        here = sub == slot
        top = (row >> 6).astype(F32)
        rest = (row & 63).astype(F32)
        high += lax.dot_general(
            hit16, jnp.where(here, top, 0.0).astype(BF16), NT, preferred_element_type=F32
        )
        low += lax.dot_general(
            hit16, jnp.where(here, rest, 0.0).astype(BF16), NT, preferred_element_type=F32
        )
    wanted_ref[...] = (high * 64.0 + low).astype(jnp.int32)


def route(owner, row):
    return pl.pallas_call(
        route_kernel,
        out_shape=(
            jax.ShapeDtypeStruct((128, 128), jnp.int32),
            jax.ShapeDtypeStruct((8, 128), jnp.int32),
        ),
        name="route",
    )(owner.reshape(8, 128), row.reshape(8, 128))


def pick_kernel(dest_ref, arrived_ref, out_ref):
    wide = lax.broadcasted_iota(jnp.int32, (256, 128 * CAP), 1)
    for b in range(WIN // 256):
        hit = (dest_ref[b * 256 : (b + 1) * 256, :] == wide).astype(F32).astype(BF16)
        out_ref[b * 256 : (b + 1) * 256, :] = jnp.dot(
            hit, arrived_ref[...], preferred_element_type=F32
        ).astype(BF16)


def pick(dest, arrived):
    return pl.pallas_call(
        pick_kernel,
        out_shape=jax.ShapeDtypeStruct((WIN, HALF), BF16),
        cost_estimate=pl.CostEstimate(
            flops=2 * WIN * 1280 * HALF, bytes_accessed=3 << 20, transcendentals=0
        ),
        name="pick",
    )(dest, arrived)


def layer_kernel(
    place_ref,
    dest_ref,
    arrived_ref,
    mine_ref,
    wq0_hbm,
    wq1_hbm,
    wo0_hbm,
    wo1_hbm,
    keep_ref,
    send_ref,
    w_ref,
    wo_ref,
    emb_ref,
    mask_ref,
    attn_ref,
    gate_ref,
    sems,
):
    c = place_ref[0]
    copies = []
    for part, src in enumerate((wq0_hbm, wq1_hbm)):
        for h in range(LOCAL):
            n = part * LOCAL + h
            copies.append(
                pltpu.make_async_copy(src.at[:, pl.ds(h * 512, 512)], w_ref.at[n], sems.at[n])
            )
    for part, src in enumerate((wo0_hbm, wo1_hbm)):
        copies.append(pltpu.make_async_copy(src, wo_ref.at[part], sems.at[8 + part]))
    for cp in copies:
        cp.start()

    mine = pl.multiple_of(c * HALF, HALF)
    other = pl.multiple_of(HALF - c * HALF, HALF)
    wide = lax.broadcasted_iota(jnp.int32, (256, 128 * CAP), 1)
    for b in range(WIN // 256):
        at = slice(b * 256, (b + 1) * 256)
        hit = (dest_ref[at, :] == wide).astype(F32).astype(BF16)
        emb_ref[at, pl.ds(other, HALF)] = jnp.dot(
            hit, arrived_ref[...], preferred_element_type=F32
        ).astype(BF16)
        emb_ref[at, pl.ds(mine, HALF)] = mine_ref[at, :]

    base = c * HALF - MAX_LEN
    for b in range(2):
        q = lax.broadcasted_iota(jnp.int32, (256, 512), 0) + (base + 256 * (b + 1))
        k = lax.broadcasted_iota(jnp.int32, (256, 512), 1) + (base + 256 * b)
        first = jnp.zeros((256, 512), jnp.int32)
        end = jnp.int32(0)
        for s in range(8):
            end = end + place_ref[1 + s]
            first = jnp.where(q >= end, end, first)
        ok = (k >= first) & (k <= q)
        mask_ref[b] = jnp.where(ok, F32(1.0 / MAX_LEN), F32(0.0))

    scale = F32(0.5 / (DH**0.5))

    def silu(x):
        h = x * F32(0.5)
        return h * (F32(1.0) + jnp.tanh(h))

    for n in range(8):
        copies[n].wait()
        w = w_ref.at[n]
        kv = silu(
            jnp.dot(emb_ref[...], w[:, DH : 3 * DH], preferred_element_type=F32)
        ).astype(BF16)
        own = emb_ref[MAX_LEN:, :]
        q = silu(jnp.dot(own, w[:, :DH], preferred_element_type=F32)).astype(BF16)
        gate_ref[:, n * DH : (n + 1) * DH] = silu(
            jnp.dot(own, w[:, 3 * DH :], preferred_element_type=F32)
        ).astype(BF16)
        for b in range(2):
            ks = kv[b * 256 : b * 256 + 512, :DH]
            vs = kv[b * 256 : b * 256 + 512, DH:]
            s = lax.dot_general(
                q[b * 256 : (b + 1) * 256], ks, NT, preferred_element_type=F32
            )
            h = s * scale
            p = (h * (F32(1.0) + jnp.tanh(h)) * mask_ref[b]).astype(BF16)
            attn_ref[b * 256 : (b + 1) * 256, n * DH : (n + 1) * DH] = jnp.dot(
                p, vs, preferred_element_type=F32
            )
    copies[8].wait()
    copies[9].wait()
    for b in range(2):
        at = slice(b * 256, (b + 1) * 256)
        attn = attn_ref[at, :]
        mean = jnp.sum(attn, axis=1, keepdims=True) * F32(1.0 / D)
        msq = jnp.sum(attn * attn, axis=1, keepdims=True) * F32(1.0 / D)
        scale_row = lax.rsqrt(msq - mean * mean + F32(1e-05))
        hidden = ((attn - mean) * scale_row * gate_ref[at, :].astype(F32)).astype(BF16)
        rows = slice(MAX_LEN + b * 256, MAX_LEN + (b + 1) * 256)
        for where, out_ref in ((other, send_ref), (mine, keep_ref)):
            mixed = jnp.dot(
                hidden[:, :HALF], wo_ref[0, :, pl.ds(where, HALF)], preferred_element_type=F32
            ) + jnp.dot(
                hidden[:, HALF:], wo_ref[1, :, pl.ds(where, HALF)], preferred_element_type=F32
            )
            out_ref[at, :] = (emb_ref[rows, pl.ds(where, HALF)].astype(F32) + mixed).astype(BF16)


def layer(place, dest, arrived, mine, wq0, wq1, wo0, wo1):
    vmem = pl.BlockSpec(memory_space=pltpu.VMEM)
    anywhere = pl.BlockSpec(memory_space=pl.ANY)
    return pl.pallas_call(
        layer_kernel,
        out_shape=(
            jax.ShapeDtypeStruct((HALF, HALF), BF16),
            jax.ShapeDtypeStruct((HALF, HALF), BF16),
        ),
        in_specs=[pl.BlockSpec(memory_space=pltpu.SMEM), vmem, vmem, vmem] + [anywhere] * 4,
        out_specs=(vmem, vmem),
        scratch_shapes=[
            pltpu.VMEM((8, D, 512), BF16),
            pltpu.VMEM((2, HALF, D), BF16),
            pltpu.VMEM((WIN, D), BF16),
            pltpu.VMEM((2, 256, 512), F32),
            pltpu.VMEM((HALF, D), F32),
            pltpu.VMEM((HALF, D), BF16),
            pltpu.SemaphoreType.DMA((10,)),
        ],
        compiler_params=pltpu.CompilerParams(vmem_limit_bytes=40 << 20),
        cost_estimate=pl.CostEstimate(
            flops=9 << 30, bytes_accessed=16 << 20, transcendentals=5 << 20
        ),
        name="layer",
    )(place, dest, arrived, mine, wq0, wq1, wo0, wo1)


def local(item_owner, item_row, seq_lengths, table, w_qkvu, w_out):
    c = lax.axis_index("col")
    swap = [(0, 1), (1, 0)]
    wanted, dest = route(item_owner, item_row)
    asked = lax.all_to_all(wanted[:, None, :], "dp", 0, 0, tiled=True)
    rows = asked[:, 0, :CAP].reshape(128 * CAP)
    fetched = table.at[rows].get(mode="promise_in_bounds")
    arrived = lax.all_to_all(fetched.reshape(128, 4 * CAP, 128), "dp", 0, 0, tiled=True)
    wq1 = lax.ppermute(w_qkvu, "col", swap)
    wo1 = lax.ppermute(w_out, "col", swap)
    padded = jnp.concatenate([jnp.full((MAX_LEN,), -1, jnp.int32), dest.reshape(TOK)])
    window = lax.dynamic_slice(padded, (c * HALF,), (WIN,)).reshape(WIN, 1)
    place = jnp.concatenate([jnp.full((1,), c, jnp.int32), seq_lengths[0]])
    theirs = lax.ppermute(arrived, "col", swap).reshape(128 * CAP, HALF)
    mine = pick(window, arrived.reshape(128 * CAP, HALF))
    keep, send = layer(place, window, theirs, mine, w_qkvu, wq1, w_out, wo1)
    got = lax.ppermute(send, "col", swap)
    first = jnp.where(c == 0, keep, got)
    second = jnp.where(c == 0, got, keep)
    return jnp.concatenate([first, second], axis=0)


def solution(mesh):
    return jax.shard_map(
        local,
        mesh=mesh,
        in_specs=(
            P("dp", None),
            P("dp"),
            P("dp", None),
            P("dp", "col"),
            P(None, "col"),
            P("col", None),
        ),
        out_specs=P("dp", "col"),
        check_vma=False,
    )
```

time: 188 us -> 116 us (0.62)
  waiting for transfers between devices: 43.8 us -> 11.4 us
  local copies, waits for them, and re-layouts: 41.8 us -> 17.4 us
  Pallas kernels: 0 us -> 23.8 us
  matrix products: 22.6 us -> 0 us
  other arithmetic: 21.3 us -> 1.22 us
  starting transfers between devices: 11.1 us -> 22.7 us
  blocking collectives: 46.4 us -> 39.5 us
    all_to_all x2 -> x1, waiting for transfers between devices: 43.8 us -> 9.64 us  [local(): asked = lax.all_to_all(wanted[:, None, :], 'dp', 0, 0, tiled=True)]
    pallas_call x0 -> x3, Pallas kernels: none -> 23.8 us  [the longest x1 17.2 us: layer(): pl.pallas_call(layer_kernel, out_shape=(jax.ShapeDtypeStruct((HALF, HALF)...]
    dot_general x3 -> x0, matrix products: 22.6 us -> none  [the longest x1 11.6 us: local(): jnp.einsum('hqk,khd->qhd', weights, values, preferred_element_type=jnp.fl...]
    convert_element_type x2 -> x0, other arithmetic: 16.8 us -> none  [local(): hidden = (normed * gates.astype(jnp.float32)).astype(jnp.bfloat16)]
    gather x4 -> x1, local copies, waits for them, and re-layouts: 15.1 us -> 6.87 us  [local(): fetched = table.at[rows].get(mode='promise_in_bounds')]
    all_to_all x4 -> x1, blocking collectives: 46.4 us -> 39.5 us  [local(): lax.all_to_all(fetched.reshape(128, 4 * CAP, 128), 'dp', 0, 0, tiled=True)]
    convert_element_type x2 -> x0, local copies, waits for them, and re-layouts: 6.6 us -> none  [local(): hidden = (normed * gates.astype(jnp.float32)).astype(jnp.bfloat16)]
    ppermute x0 -> x4, starting transfers between devices: none -> 6.33 us  [the longest x1 4.65 us: local(): theirs = lax.ppermute(arrived, 'col', swap).reshape(128 * CAP, HALF)]
  transfers between devices with their start and end apart: 2 -> 5, of which waited for: 1 -> 2; matrix products, arithmetic and copies ran while one was open for 7% -> 12% of each run, Pallas kernels for 0% -> 3%
where the time goes in v1:
time: 116 us
  blocking collectives  39.5 us (34%)
  Pallas kernels  23.8 us (21%)
  starting transfers between devices  22.7 us (20%)
  local copies, waits for them, and re-layouts  17.4 us (15%)
  waiting for transfers between devices  11.4 us (10%)
  other arithmetic  1.22 us (1%)
    all_to_all x1, blocking collectives, local(): lax.all_to_all(fetched.reshape(128, 4 * CAP, 128), 'dp', 0, 0, tiled=True)  39.5 us
    pallas_call x1, Pallas kernels, layer(): pl.pallas_call(layer_kernel, out_shape=(jax.ShapeDtypeStruct((HALF, HALF)...  17.2 us
    all_to_all x1, starting transfers between devices, local(): asked = lax.all_to_all(wanted[:, None, :], 'dp', 0, 0, tiled=True)  16.3 us
    all_to_all x1, waiting for transfers between devices, local(): asked = lax.all_to_all(wanted[:, None, :], 'dp', 0, 0, tiled=True)  9.64 us
    gather x1, local copies, waits for them, and re-layouts, local(): fetched = table.at[rows].get(mode='promise_in_bounds')  6.87 us
    ppermute x1, starting transfers between devices, local(): theirs = lax.ppermute(arrived, 'col', swap).reshape(128 * CAP, HALF)  4.65 us
    pallas_call x1, Pallas kernels, pick(): pl.pallas_call(pick_kernel, out_shape=jax.ShapeDtypeStruct((WIN, HALF), B...  3.6 us
    unnamed x12, local copies, waits for them, and re-layouts  3.33 us
  transfers between devices with their start and end apart: 5, of which 2 were waited for; matrix products, arithmetic and copies ran while one was open for 12% of the time, Pallas kernels for 3%

profile of v1, /device:TPU:1, one launch (start us, length us, event | category | flops | bytes accessed | tf_op | source)
XLA Modules:
  0.0 116.0 jit_solution(16563900717502309847)
XLA Ops:
  0.0 3.0 %route.1 = (s32[128,128]{1,0:T(8,128)}, s32[8,128]{1,0:T(8,128)}) custom-call(s32[8,128]{1,0:T(8,128)} %bitcast.9, s32[8,128]{1,0:T(8,128)} %bitcast.10), custom_call_target="tpu_custom_call" | custom-call | tf_op jit(solution)/shard_map/route/pallas_call | solution.py:50
  3.0 16.3 %all-to-all-start = ((s32[128,1,128]{2,1,0:T(1,128)}), s32[128,1,128]{2,1,0:T(1,128)S(1)}, u32[]{:S(2)}, u32[]{:S(2)}) async-start(s32[128,1,128]{2,1,0:T(1,128)} %bitcast.8), calls=%async_computation | async-start | bytes 131072 | tf_op jit(solution)/shard_map/all_to_all | solution.py:214
  19.3 1.0 collective-permute-start.1
  20.3 9.6 %all-to-all-done = s32[128,1,128]{2,1,0:T(1,128)S(1)} async-done(((s32[128,1,128]{2,1,0:T(1,128)}), s32[128,1,128]{2,1,0:T(1,128)S(1)}, u32[]{:S(2)}, u32[]{:S(2)}) %all-to-all-start) | async-done | bytes 65568 | tf_op jit(solution)/shard_map/all_to_all | solution.py:214
  30.0 0.2 slice_reduce_fusion
  30.2 0.1 reshape_squeeze.3
  30.4 6.9 %gather_fusion = bf16[1280,512]{1,0:T(8,128)(2,1)S(1)} fusion(bf16[4096,512]{1,0:T(8,128)(2,1)} %param.9, s32[2048]{0:T(1024)S(1)} %pad_clamp_fusion), kind=kCustom, calls=%fused_computation | custom fusion | bytes 2626560 | tf_op jit(solution)/shard_map/gather | solution.py:216
  37.2 1.7 %reshape.53 = bf16[128,40,128]{2,1,0:T(8,128)(2,1)} reshape(bf16[1280,512]{1,0:T(8,128)(2,1)S(1)} %gather_fusion) | data formatting | bytes 2621440 | tf_op jit(solution)/shard_map/reshape | solution.py:217
  38.9 39.5 %all_to_all.10 = bf16[128,40,128]{2,1,0:T(8,128)(2,1)S(1)} all-to-all(bf16[128,40,128]{2,1,0:T(8,128)(2,1)} %reshape.53), channel_id=1, replica_groups=mesh['dp'=128,'col'=2] {'dp'}, dimensions={0} | all-to-all | bytes 2621440 | tf_op jit(solution)/shard_map/all_to_all | solution.py:217
  78.4 4.7 %collective-permute-start = (bf16[128,40,128]{2,1,0:T(8,128)(2,1)S(1)}, bf16[128,40,128]{2,1,0:T(8,128)(2,1)}, u32[]{:S(2)}, u32[]{:S(2)}) collective-permute-start(bf16[128,40,128]{2,1,0:T(8,128)(2,1)S(1)} %all_to_all.10), channel_id=1, source_target_pairs={{0,1},{1,0},{2,3},{3,2},{4,5},{5,4},{6,7},{7,6},{8,9},{9,8},{10,11... | collective-permute-start | bytes 3932168 | tf_op jit(solution)/shard_map/ppermute | solution.py:223
  83.1 0.1 pad_dynamic-slice_fusion
  83.2 0.9 reshape.64.dest_ref
  84.1 0.1 pad_add_fusion.place_ref
  84.2 1.6 %reshape.55.arrived_ref = bf16[1280,512]{1,0:T(8,128)(2,1)} reshape(bf16[128,40,128]{2,1,0:T(8,128)(2,1)S(1)} %all_to_all.10) | data formatting | bytes 2621440 | tf_op jit(solution)/shard_map/reshape | solution.py:224
  85.8 3.6 %pick.1.mine_ref = bf16[768,512]{1,0:T(8,128)(2,1)} custom-call(s32[768,1]{1,0:T(8,128)} %reshape.64.dest_ref, bf16[1280,512]{1,0:T(8,128)(2,1)} %reshape.55.arrived_ref), custom_call_target="tpu_custom_call" | custom-call | flops 1006632960 | bytes 3145728 | tf_op jit(solution)/shard_map/pick/pallas_call | solution.py:70
  89.4 2.5 %reshape.54.arrived_ref = bf16[1280,512]{1,0:T(8,128)(2,1)S(1)} reshape(bf16[128,40,128]{2,1,0:T(8,128)(2,1)} %collective-permute-done) | data formatting | bytes 2621440 | tf_op jit(solution)/shard_map/reshape | solution.py:223
  92.0 0.0 copy-start.1
  92.0 2.2 %copy-done.1 = bf16[1024,2048]{1,0:T(8,128)(2,1)S(1)} copy-done((bf16[1024,2048]{1,0:T(8,128)(2,1)S(1)}, bf16[1024,2048]{1,0:T(8,128)(2,1)}, u32[]{:S(2)}) %copy-start.1) | copy-done | bytes 4194328
  94.2 1.1 copy-done.3
  95.3 17.2 %layer.1 = (bf16[512,512]{1,0:T(8,128)(2,1)S(1)}, bf16[512,512]{1,0:T(8,128)(2,1)}) custom-call(s32[9]{0:T(128)S(1)} %pad_add_fusion.place_ref, s32[768,1]{1,0:T(8,128)S(1)} %copy-done, bf16[1280,512]{1,0:T(8,128)(2,1)S(1)} %reshape.54.arrived_ref, bf16[768,512]{1,0:T(8,128)(2,1)S(1)} %copy-done.3, bf16[1024,2048]{1,0:T(8,128)(2,1)S(1)} %copy-done.1, ...), custom_call_target="tpu_custom_call" | custom-call | flops 9663676416 | bytes 16777216 | tf_op jit(solution)/shard_map/layer/pallas_call | solution.py:185
  112.5 0.6 collective-permute-start.3
  113.2 1.7 %collective-permute-done.3 = bf16[512,512]{1,0:T(8,128)(2,1)S(1)} collective-permute-done((bf16[512,512]{1,0:T(8,128)(2,1)}, bf16[512,512]{1,0:T(8,128)(2,1)S(1)}, u32[]{:S(2)}, u32[]{:S(2)}) %collective-permute-start.3) | collective-permute-done | bytes 524320 | tf_op jit(solution)/shard_map/ppermute | solution.py:226
  114.9 0.1 broadcast_select_fusion.1
  115.0 1.0 pad_maximum_fusion
  (15 shorter events, 0.1 us)
Async XLA Ops:
  3.0 27.0 %all-to-all-start = ((s32[128,1,128]{2,1,0:T(1,128)}), s32[128,1,128]{2,1,0:T(1,128)S(1)}, u32[]{:S(2)}, u32[]{:S(2)}) async-start(s32[128,1,128]{2,1,0:T(1,128)} %bitcast.8), calls=%async_computation | async-start | bytes 131072 | tf_op jit(solution)/shard_map/all_to_all | solution.py:214
  19.3 72.7 %collective-permute-start.1 = (bf16[1024,2048]{1,0:T(8,128)(2,1)}, bf16[1024,2048]{1,0:T(8,128)(2,1)}, u32[]{:S(2)}, u32[]{:S(2)}) collective-permute-start(bf16[1024,2048]{1,0:T(8,128)(2,1)} %wq0_hbm.1), channel_id=1, source_target_pairs={{0,1},{1,0},{2,3},{3,2},{4,5},{5,4},{6,7},{7,6},{8,9},{9,8},{10,11... | collective-permute-start | bytes 12582920 | tf_op jit(solution)/shard_map/ppermute | solution.py:218
  38.9 44.2 %copy-start.2 = (bf16[512,1024]{1,0:T(8,128)(2,1)S(1)}, bf16[512,1024]{1,0:T(8,128)(2,1)}, u32[]{:S(2)}) copy-start(bf16[512,1024]{1,0:T(8,128)(2,1)} %wo0_hbm.1) | copy-start | bytes 3145732
  38.9 44.2 %copy-start.4 = (s32[8,128]{1,0:T(8,128)S(1)}, s32[8,128]{1,0:T(8,128)}, u32[]{:S(2)}) copy-start(s32[8,128]{1,0:T(8,128)} %get-tuple-element.9) | copy-start | bytes 12292
  38.9 45.2 %copy-start.5 = (s32[1,8]{1,0:T(1,128)S(1)}, s32[1,8]{1,0:T(1,128)}, u32[]{:S(2)}) copy-start(s32[1,8]{1,0:T(1,128)} %param.8) | copy-start | bytes 100
  78.4 11.0 %collective-permute-start = (bf16[128,40,128]{2,1,0:T(8,128)(2,1)S(1)}, bf16[128,40,128]{2,1,0:T(8,128)(2,1)}, u32[]{:S(2)}, u32[]{:S(2)}) collective-permute-start(bf16[128,40,128]{2,1,0:T(8,128)(2,1)S(1)} %all_to_all.10), channel_id=1, source_target_pairs={{0,1},{1,0},{2,3},{3,2},{4,5},{5,4},{6,7},{7,6},{8,9},{9,8},{10,11... | collective-permute-start | bytes 3932168 | tf_op jit(solution)/shard_map/ppermute | solution.py:223
  83.1 8.9 %collective-permute-start.2 = (bf16[512,1024]{1,0:T(8,128)(2,1)S(1)}, bf16[512,1024]{1,0:T(8,128)(2,1)}, u32[]{:S(2)}, u32[]{:S(2)}) collective-permute-start(bf16[512,1024]{1,0:T(8,128)(2,1)S(1)} %copy-done.2), channel_id=1, source_target_pairs={{0,1},{1,0},{2,3},{3,2},{4,5},{5,4},{6,7},{7,6},{8,9},{9,8},{10,11... | collective-permute-start | bytes 3145736 | tf_op jit(solution)/shard_map/ppermute | solution.py:219
  89.4 2.6 %copy-start = (s32[768,1]{1,0:T(8,128)S(1)}, s32[768,1]{1,0:T(8,128)}, u32[]{:S(2)}) copy-start(s32[768,1]{1,0:T(8,128)} %reshape.64.dest_ref) | copy-start | bytes 9220
  92.0 2.2 %copy-start.1 = (bf16[1024,2048]{1,0:T(8,128)(2,1)S(1)}, bf16[1024,2048]{1,0:T(8,128)(2,1)}, u32[]{:S(2)}) copy-start(bf16[1024,2048]{1,0:T(8,128)(2,1)} %wq0_hbm.1) | copy-start | bytes 12582916
  94.2 1.1 copy-start.3
  112.5 2.4 %collective-permute-start.3 = (bf16[512,512]{1,0:T(8,128)(2,1)}, bf16[512,512]{1,0:T(8,128)(2,1)S(1)}, u32[]{:S(2)}, u32[]{:S(2)}) collective-permute-start(bf16[512,512]{1,0:T(8,128)(2,1)} %get-tuple-element.12), channel_id=1, source_target_pairs={{0,1},{1,0},{2,3},{3,2},{4,5},{5,4},{6,7},{7,6},{8,9},{9,8},{10,11... | collective-permute-start | bytes 1572872 | tf_op jit(solution)/shard_map/ppermute | solution.py:226

commit v2 on v1

v2 whole, which is shorter than its diff:
```python
import jax
import jax.numpy as jnp
from jax import lax
from jax.experimental import pallas as pl
from jax.experimental.pallas import tpu as pltpu
from jax.sharding import PartitionSpec as P

D = 1024
DH = 128
MAX_LEN = 256
TOK = 1024
HALF = 512
CAP = 10
WIN = HALF + MAX_LEN
LOCAL = 4
F32 = jnp.float32
BF16 = jnp.bfloat16
NT = (((1,), (1,)), ((), ()))


def route_kernel(owner_ref, row_ref, wanted_ref, dest_ref):
    sub = lax.broadcasted_iota(jnp.int32, (128, 128), 0)
    lane = lax.broadcasted_iota(jnp.int32, (128, 128), 1)
    before = (sub < lane).astype(F32).astype(BF16)
    count = jnp.zeros((128, 1), F32)
    high = jnp.zeros((128, 128), F32)
    low = jnp.zeros((128, 128), F32)
    for b in range(TOK // 128):
        owner = owner_ref[b : b + 1, :]
        row = row_ref[b : b + 1, :]
        hit = (sub == owner).astype(F32)
        hit16 = hit.astype(BF16)
        rank = jnp.dot(hit16, before, preferred_element_type=F32) + count
        slot = jnp.sum(hit * rank, axis=0, keepdims=True).astype(jnp.int32)
        count = count + jnp.sum(hit, axis=1, keepdims=True)
        dest_ref[b : b + 1, :] = owner * CAP + slot
        here = sub == slot
        spot = ((row >> 3) << 5) + (row & 7)
        top = (spot >> 6).astype(F32)
        rest = (spot & 63).astype(F32)
        high += lax.dot_general(
            hit16, jnp.where(here, top, 0.0).astype(BF16), NT, preferred_element_type=F32
        )
        low += lax.dot_general(
            hit16, jnp.where(here, rest, 0.0).astype(BF16), NT, preferred_element_type=F32
        )
    wanted_ref[...] = (high * 64.0 + low).astype(jnp.int32)


def route(owner, row):
    return pl.pallas_call(
        route_kernel,
        out_shape=(
            jax.ShapeDtypeStruct((128, 128), jnp.int32),
            jax.ShapeDtypeStruct((8, 128), jnp.int32),
        ),
        name="route",
    )(owner.reshape(8, 128), row.reshape(8, 128))


def fetch_kernel(asked_ref, table_ref, out_ref, tall_ref, wide_ref):
    def widen(j, _):
        at = pl.ds(pl.multiple_of(j * 16, 16), 16)
        for k in range(4):
            v = table_ref[at, k * 128 : (k + 1) * 128].astype(F32)
            tall_ref[pl.ds(pl.multiple_of(j * 64 + k * 8, 8), 8), :] = v[:8]
            tall_ref[pl.ds(pl.multiple_of(j * 64 + 32 + k * 8, 8), 8), :] = v[8:]
        return 0

    lax.fori_loop(0, 4096 // 16, widen, 0, unroll=4)

    def body(g, _):
        for s in range(CAP):
            at = asked_ref[g, s]
            wide_ref[pl.ds(g * 40 + 4 * s, 4), :] = tall_ref[pl.ds(at, 4, stride=8), :]
        return 0

    lax.fori_loop(0, 128, body, 0, unroll=2)
    out_ref[...] = wide_ref[...].astype(BF16)


def fetch(asked, table):
    return pl.pallas_call(
        fetch_kernel,
        out_shape=jax.ShapeDtypeStruct((128 * 40, 128), BF16),
        in_specs=[
            pl.BlockSpec(memory_space=pltpu.SMEM),
            pl.BlockSpec(memory_space=pltpu.VMEM),
        ],
        out_specs=pl.BlockSpec(memory_space=pltpu.VMEM),
        scratch_shapes=[
            pltpu.VMEM((4096 * 4, 128), F32),
            pltpu.VMEM((128 * 40, 128), F32),
        ],
        compiler_params=pltpu.CompilerParams(vmem_limit_bytes=18 << 20),
        name="fetch",
    )(asked, table)


def place_kernel(
    place_ref, dest_ref, arrived_ref, w_hbm, mine_ref, send_ref, held_hbm, wide_ref, emb_ref
):
    wide_ref[...] = arrived_ref[...].astype(F32)

    def body(j, _):
        for r in range(8):
            at = dest_ref[j * 8 + r]
            emb_ref[pl.ds(MAX_LEN * 4 + j * 32 + r, 4, stride=8), :] = wide_ref[
                pl.ds(pl.multiple_of(at * 4, 4), 4), :
            ]
        return 0

    lax.fori_loop(0, TOK // 8, body, 0, unroll=2)
    emb_ref[: MAX_LEN * 4, :] = jnp.zeros((MAX_LEN * 4, 128), F32)
    c = place_ref[0]

    def window(out_ref, base):
        def body(m, _):
            rows = pl.ds(pl.multiple_of(m * 16, 16), 16)
            for k in range(4):
                lo = emb_ref[pl.ds(pl.multiple_of(base + m * 64 + k * 8, 8), 8), :]
                hi = emb_ref[pl.ds(pl.multiple_of(base + m * 64 + 32 + k * 8, 8), 8), :]
                out_ref[rows, k * 128 : (k + 1) * 128] = jnp.concatenate(
                    [lo, hi], axis=0
                ).astype(BF16)
            return 0

        lax.fori_loop(0, WIN // 16, body, 0, unroll=4)

    window(send_ref, pl.multiple_of((1 - c) * HALF * 4, HALF * 4))
    window(mine_ref, pl.multiple_of(c * HALF * 4, HALF * 4))


def put(place, dest, arrived, w):
    vmem = pl.BlockSpec(memory_space=pltpu.VMEM)
    smem = pl.BlockSpec(memory_space=pltpu.SMEM)
    return pl.pallas_call(
        place_kernel,
        out_shape=(
            jax.ShapeDtypeStruct((WIN, HALF), BF16),
            jax.ShapeDtypeStruct((WIN, HALF), BF16),
            jax.ShapeDtypeStruct((D, 4 * HALF), BF16),
        ),
        in_specs=[smem, smem, vmem, pl.BlockSpec(memory_space=pltpu.HBM)],
        out_specs=(vmem, vmem, pl.BlockSpec(memory_space=pltpu.HBM)),
        input_output_aliases={3: 2},
        scratch_shapes=[
            pltpu.VMEM((128 * 40, 128), F32),
            pltpu.VMEM(((TOK + MAX_LEN) * 4, 128), F32),
        ],
        compiler_params=pltpu.CompilerParams(vmem_limit_bytes=12 << 20),
        name="put",
    )(place, dest, arrived, w)


def silu(x):
    h = x * F32(0.5)
    return h * (F32(1.0) + jnp.tanh(h))


def layer_kernel(
    place_ref,
    lengths_ref,
    mine_ref,
    theirs_ref,
    wq0_ref,
    wq1_hbm,
    wo0_hbm,
    wo1_hbm,
    send_ref,
    hidden_ref,
    kv_ref,
    qu_ref,
    emb_ref,
    w_ref,
    wo_ref,
    mask_ref,
    attn_ref,
    gate_ref,
    sems,
):
    c = place_ref[0]
    other = pl.multiple_of(HALF - c * HALF, HALF)
    copies = [
        pltpu.make_async_copy(
            wq1_hbm.at[:, pl.ds(h * 512, 512)], w_ref.at[h], sems.at[h]
        )
        for h in range(LOCAL)
    ]
    for part, src in enumerate((wo0_hbm, wo1_hbm)):
        copies.append(
            pltpu.make_async_copy(
                src.at[:, pl.ds(other, HALF)],
                wo_ref.at[pl.ds(part * HALF, HALF)],
                sems.at[LOCAL + part],
            )
        )
    for cp in copies:
        cp.start()

    @pl.when(c == 0)
    def _():
        emb_ref[:, :HALF] = mine_ref[...]
        emb_ref[:, HALF:] = theirs_ref[...]

    @pl.when(c != 0)
    def _():
        emb_ref[:, :HALF] = theirs_ref[...]
        emb_ref[:, HALF:] = mine_ref[...]

    base = c * HALF - MAX_LEN
    for b in range(2):
        q = lax.broadcasted_iota(jnp.int32, (256, 1), 0) + (base + 256 * (b + 1))
        k = lax.broadcasted_iota(jnp.int32, (256, 512), 1) + (base + 256 * b)
        first = jnp.zeros((256, 1), jnp.int32)
        end = jnp.int32(0)
        for s in range(8):
            end = end + lengths_ref[0, s]
            first = jnp.where(q >= end, end, first)
        ok = (k >= first) & (k <= q)
        mask_ref[b] = jnp.where(ok, F32(1.0 / MAX_LEN), F32(0.0))

    scale = F32(0.5 / (DH**0.5))
    def attend(n, qu, kv):
        for b in range(2):
            ks = kv[b * 256 : b * 256 + 512, :DH]
            vs = kv[b * 256 : b * 256 + 512, DH:]
            s = lax.dot_general(
                qu[b * 256 : (b + 1) * 256, :DH], ks, NT, preferred_element_type=F32
            )
            h = s * scale
            p = (h * (F32(1.0) + jnp.tanh(h)) * mask_ref[b]).astype(BF16)
            attn_ref[b * 256 : (b + 1) * 256, n * DH : (n + 1) * DH] = jnp.dot(
                p, vs, preferred_element_type=F32
            )

    for n in range(9):
        if n < 8:
            if n < LOCAL:
                w = wq0_ref.at[:, n * 512 : (n + 1) * 512]
            else:
                copies[n - LOCAL].wait()
                w = w_ref.at[n - LOCAL]
            kv_ref[n % 2] = silu(
                jnp.dot(emb_ref[...], w[:, DH : 3 * DH], preferred_element_type=F32)
            ).astype(BF16)
        if n > 0:
            attend(n - 1, qu_ref[(n - 1) % 2], kv_ref[(n - 1) % 2])
        if n < 8:
            ends = jnp.concatenate([w[:, :DH], w[:, 3 * DH :]], axis=1)
            qu = silu(
                jnp.dot(emb_ref[MAX_LEN:, :], ends, preferred_element_type=F32)
            ).astype(BF16)
            qu_ref[n % 2] = qu
            gate_ref[:, n * DH : (n + 1) * DH] = qu[:, DH:]
    copies[LOCAL].wait()
    copies[LOCAL + 1].wait()
    for b in range(2):
        at = slice(b * 256, (b + 1) * 256)
        attn = attn_ref[at, :]
        mean = jnp.sum(attn, axis=1, keepdims=True) * F32(1.0 / D)
        msq = jnp.sum(attn * attn, axis=1, keepdims=True) * F32(1.0 / D)
        scale_row = lax.rsqrt(msq - mean * mean + F32(1e-05))
        hidden = ((attn - mean) * scale_row * gate_ref[at, :].astype(F32)).astype(BF16)
        hidden_ref[at, :] = hidden
        mixed = jnp.dot(hidden, wo_ref[...], preferred_element_type=F32)
        emb = theirs_ref[MAX_LEN + b * 256 : MAX_LEN + (b + 1) * 256, :].astype(F32)
        send_ref[at, :] = (emb + mixed).astype(BF16)


def layer(place, lengths, mine, theirs, wq0, wq1, wo0, wo1):
    vmem = pl.BlockSpec(memory_space=pltpu.VMEM)
    hbm = pl.BlockSpec(memory_space=pltpu.HBM)
    smem = pl.BlockSpec(memory_space=pltpu.SMEM)
    return pl.pallas_call(
        layer_kernel,
        out_shape=(
            jax.ShapeDtypeStruct((HALF, HALF), BF16),
            jax.ShapeDtypeStruct((HALF, D), BF16),
        ),
        in_specs=[smem, smem, vmem, vmem, vmem] + [hbm] * 3,
        out_specs=(vmem, vmem),
        scratch_shapes=[
            pltpu.VMEM((2, WIN, 256), BF16),
            pltpu.VMEM((2, HALF, 256), BF16),
            pltpu.VMEM((WIN, D), BF16),
            pltpu.VMEM((LOCAL, D, 512), BF16),
            pltpu.VMEM((D, HALF), BF16),
            pltpu.VMEM((2, 256, 512), F32),
            pltpu.VMEM((HALF, D), F32),
            pltpu.VMEM((HALF, D), BF16),
            pltpu.SemaphoreType.DMA((LOCAL + 2,)),
        ],
        compiler_params=pltpu.CompilerParams(vmem_limit_bytes=30 << 20),
        cost_estimate=pl.CostEstimate(
            flops=7 << 30, bytes_accessed=12 << 20, transcendentals=5 << 20
        ),
        name="layer",
    )(place, lengths, mine, theirs, wq0, wq1, wo0, wo1)


def keep_kernel(
    place_ref, hidden_ref, mine_ref, wo0_hbm, wo1_hbm, out_hbm, wo_ref, out_ref, sems
):
    mine = pl.multiple_of(place_ref[0] * HALF, HALF)
    copies = [
        pltpu.make_async_copy(
            src.at[:, pl.ds(mine, HALF)], wo_ref.at[pl.ds(part * HALF, HALF)], sems.at[part]
        )
        for part, src in enumerate((wo0_hbm, wo1_hbm))
    ]
    for cp in copies:
        cp.start()
    for cp in copies:
        cp.wait()
    mixed = jnp.dot(hidden_ref[...], wo_ref[...], preferred_element_type=F32)
    out_ref[...] = (mine_ref[MAX_LEN:, :].astype(F32) + mixed).astype(BF16)
    done = pltpu.make_async_copy(out_ref, out_hbm.at[pl.ds(mine, HALF), :], sems.at[2])
    done.start()
    done.wait()


def keep(place, hidden, mine, wo0, wo1):
    vmem = pl.BlockSpec(memory_space=pltpu.VMEM)
    hbm = pl.BlockSpec(memory_space=pltpu.HBM)
    return pl.pallas_call(
        keep_kernel,
        out_shape=jax.ShapeDtypeStruct((TOK, HALF), BF16),
        in_specs=[pl.BlockSpec(memory_space=pltpu.SMEM), vmem, vmem, hbm, hbm],
        out_specs=hbm,
        scratch_shapes=[
            pltpu.VMEM((D, HALF), BF16),
            pltpu.VMEM((HALF, HALF), BF16),
            pltpu.SemaphoreType.DMA((3,)),
        ],
        compiler_params=pltpu.CompilerParams(vmem_limit_bytes=10 << 20),
        cost_estimate=pl.CostEstimate(
            flops=1 << 29, bytes_accessed=3 << 20, transcendentals=0
        ),
        name="keep",
    )(place, hidden, mine, wo0, wo1)


def join_kernel(place_ref, got_ref, half_hbm, out_hbm, sem):
    other = pl.multiple_of(HALF - place_ref[0] * HALF, HALF)
    done = pltpu.make_async_copy(got_ref, out_hbm.at[pl.ds(other, HALF), :], sem)
    done.start()
    done.wait()


def join(place, got, half):
    hbm = pl.BlockSpec(memory_space=pltpu.HBM)
    return pl.pallas_call(
        join_kernel,
        out_shape=jax.ShapeDtypeStruct((TOK, HALF), BF16),
        in_specs=[
            pl.BlockSpec(memory_space=pltpu.SMEM),
            pl.BlockSpec(memory_space=pltpu.VMEM),
            hbm,
        ],
        out_specs=hbm,
        scratch_shapes=[pltpu.SemaphoreType.DMA],
        input_output_aliases={2: 0},
        compiler_params=pltpu.CompilerParams(vmem_limit_bytes=4 << 20),
        name="join",
    )(place, got, half)


def local(item_owner, item_row, seq_lengths, table, w_qkvu, w_out):
    c = lax.axis_index("col")
    swap = [(0, 1), (1, 0)]
    wanted, dest = route(item_owner, item_row)
    asked = lax.all_to_all(wanted[:, None, :], "dp", 0, 0, tiled=True)
    wq1 = lax.ppermute(w_qkvu, "col", swap)
    wo1 = lax.ppermute(w_out, "col", swap)
    place = jnp.reshape(c, (1,)).astype(jnp.int32)
    dest = dest.reshape(TOK)
    asked, wq1, wo1 = lax.optimization_barrier((asked, wq1, wo1))
    fetched = fetch(asked[:, 0, :], table)
    arrived = lax.all_to_all(fetched.reshape(128, 4 * CAP, 128), "dp", 0, 0, tiled=True)
    mine, send, held = put(place, dest, arrived.reshape(128 * 4 * CAP, 128), wq1)
    theirs = lax.ppermute(send, "col", swap)
    out, hidden = layer(place, seq_lengths, mine, theirs, w_qkvu, held, w_out, wo1)
    got = lax.ppermute(out, "col", swap)
    half = keep(place, hidden, mine, w_out, wo1)
    return join(place, got, half)


def solution(mesh):
    return jax.shard_map(
        local,
        mesh=mesh,
        in_specs=(
            P("dp", None),
            P("dp"),
            P("dp", None),
            P("dp", "col"),
            P(None, "col"),
            P("col", None),
        ),
        out_specs=P("dp", "col"),
        check_vma=False,
    )
```

time: 116 us -> 102 us (0.88)
  waiting for transfers between devices: 11.4 us -> 34.8 us
  local copies, waits for them, and re-layouts: 17.4 us -> 2.2 us
  blocking collectives: 39.5 us -> 24.6 us
  starting transfers between devices: 22.7 us -> 14.8 us
  Pallas kernels: 23.8 us -> 25.2 us
  other arithmetic: 1.22 us -> 0 us
    all_to_all x1, waiting for transfers between devices: 9.64 us -> 32.9 us  [local(): lax.all_to_all(fetched.reshape(128, 4 * CAP, 128), 'dp', 0, 0, tiled=True)]
    all_to_all x1, blocking collectives: 39.5 us -> 24.6 us  [local(): asked = lax.all_to_all(wanted[:, None, :], 'dp', 0, 0, tiled=True)]
    all_to_all x1, starting transfers between devices: 16.3 us -> 6.33 us  [local(): lax.all_to_all(fetched.reshape(128, 4 * CAP, 128), 'dp', 0, 0, tiled=True)]
    gather x1 -> x0, local copies, waits for them, and re-layouts: 6.87 us -> none  [local(): fetched = table.at[rows].get(mode='promise_in_bounds')]
    reshape x4 -> x0, local copies, waits for them, and re-layouts: 6.81 us -> none  [the longest x1 2.55 us: local(): theirs = lax.ppermute(arrived, 'col', swap).reshape(128 * CAP, HALF)]
    pallas_call x1 -> x4, Pallas kernels: 3.6 us -> 10.3 us  [the longest x1 5.11 us: fetch(): pl.pallas_call(fetch_kernel, out_shape=jax.ShapeDtypeStruct((128 * 40, 12...]
    pallas_call x1, Pallas kernels: 17.2 us -> 11.9 us  [layer(): pl.pallas_call(layer_kernel, out_shape=(jax.ShapeDtypeStruct((HALF, HALF)...]
    ppermute x1, starting transfers between devices: 1.05 us -> 3.2 us  [local(): wq1 = lax.ppermute(w_qkvu, 'col', swap)]
  transfers between devices with their start and end apart: 5 -> 5, of which waited for: 2 -> 2; matrix products, arithmetic and copies ran while one was open for 12% -> 0% of each run, Pallas kernels for 3% -> 5%
where the time goes in v2:
time: 102 us
  waiting for transfers between devices  34.8 us (34%)
  Pallas kernels  25.2 us (25%)
  blocking collectives  24.6 us (24%)
  starting transfers between devices  14.8 us (15%)
  local copies, waits for them, and re-layouts  2.2 us (2%)
    all_to_all x1, waiting for transfers between devices, local(): lax.all_to_all(fetched.reshape(128, 4 * CAP, 128), 'dp', 0, 0, tiled=True)  32.9 us
    all_to_all x1, blocking collectives, local(): asked = lax.all_to_all(wanted[:, None, :], 'dp', 0, 0, tiled=True)  24.6 us
    pallas_call x1, Pallas kernels, layer(): pl.pallas_call(layer_kernel, out_shape=(jax.ShapeDtypeStruct((HALF, HALF)...  11.9 us
    all_to_all x1, starting transfers between devices, local(): lax.all_to_all(fetched.reshape(128, 4 * CAP, 128), 'dp', 0, 0, tiled=True)  6.33 us
    pallas_call x1, Pallas kernels, fetch(): pl.pallas_call(fetch_kernel, out_shape=jax.ShapeDtypeStruct((128 * 40, 12...  5.11 us
    ppermute x1, starting transfers between devices, local(): theirs = lax.ppermute(send, 'col', swap)  4.76 us
    ppermute x1, starting transfers between devices, local(): wq1 = lax.ppermute(w_qkvu, 'col', swap)  3.2 us
    pallas_call x1, Pallas kernels, route(): pl.pallas_call(route_kernel, out_shape=(jax.ShapeDtypeStruct((128, 128),...  2.96 us
  transfers between devices with their start and end apart: 5, of which 2 were waited for; matrix products, arithmetic and copies ran while one was open for 0% of the time, Pallas kernels for 5%

profile of v2, /device:TPU:1, one launch (start us, length us, event | category | flops | bytes accessed | tf_op | source)
XLA Modules:
  0.0 101.8 jit_solution(16954888760985338217)
XLA Ops:
  0.0 3.2 %collective-permute-start = (bf16[1024,2048]{1,0:T(8,128)(2,1)}, bf16[1024,2048]{1,0:T(8,128)(2,1)}, u32[]{:S(2)}, u32[]{:S(2)}) collective-permute-start(bf16[1024,2048]{1,0:T(8,128)(2,1)} %wq0_ref.1), channel_id=1, source_target_pairs={{0,1},{1,0},{2,3},{3,2},{4,5},{5,4},{6,7},{7,6},{8,9},{9,8},{10,11... | collective-permute-start | bytes 12582920 | tf_op jit(solution)/shard_map/ppermute | solution.py:374
  3.2 0.0 collective-permute-start.1
  3.2 3.0 %route.1 = (s32[128,128]{1,0:T(8,128)}, s32[8,128]{1,0:T(8,128)}) custom-call(s32[8,128]{1,0:T(8,128)} %bitcast.14, s32[8,128]{1,0:T(8,128)} %bitcast.15), custom_call_target="tpu_custom_call" | custom-call | tf_op jit(solution)/shard_map/route/pallas_call | solution.py:51
  6.2 0.0 copy-start.2
  6.2 24.6 %all_to_all.10 = s32[128,1,128]{2,1,0:T(1,128)S(1)} all-to-all(s32[128,1,128]{2,1,0:T(1,128)} %bitcast.13), channel_id=1, replica_groups=mesh['dp'=128,'col'=2] {'dp'}, dimensions={0} | all-to-all | bytes 131072 | tf_op jit(solution)/shard_map/all_to_all | solution.py:373
  30.8 0.0 collective-permute-done.1.wo1_hbm
  30.8 0.0 collective-permute-done.w_hbm
  30.8 0.0 copy-start
  30.8 2.2 %copy-done = bf16[4096,512]{1,0:T(8,128)(2,1)S(1)} copy-done((bf16[4096,512]{1,0:T(8,128)(2,1)S(1)}, bf16[4096,512]{1,0:T(8,128)(2,1)}, u32[]{:S(2)}) %copy-start) | copy-done | bytes 4194328
  33.0 5.1 %fetch.1 = bf16[5120,128]{1,0:T(8,128)(2,1)} custom-call(s32[128,128]{1,0:T(8,128)S(1)} %bitcast.11, bf16[4096,512]{1,0:T(8,128)(2,1)S(1)} %copy-done), custom_call_target="tpu_custom_call" | custom-call | tf_op jit(solution)/shard_map/fetch/pallas_call | solution.py:83
  38.1 6.3 %all-to-all-start.1 = ((bf16[128,40,128]{2,1,0:T(8,128)(2,1)}), bf16[128,40,128]{2,1,0:T(8,128)(2,1)S(1)}, u32[]{:S(2)}, u32[]{:S(2)}) async-start(bf16[128,40,128]{2,1,0:T(8,128)(2,1)} %bitcast.7), calls=%async_computation.1 | async-start | bytes 2621440 | tf_op jit(solution)/shard_map/all_to_all | solution.py:380
  44.4 32.9 %all-to-all-done.1 = bf16[128,40,128]{2,1,0:T(8,128)(2,1)S(1)} async-done(((bf16[128,40,128]{2,1,0:T(8,128)(2,1)}), bf16[128,40,128]{2,1,0:T(8,128)(2,1)S(1)}, u32[]{:S(2)}, u32[]{:S(2)}) %all-to-all-start.1) | async-done | bytes 1310752 | tf_op jit(solution)/shard_map/all_to_all | solution.py:380
  77.3 0.0 copy-done.2
  77.3 2.7 %put.1 = (bf16[768,512]{1,0:T(8,128)(2,1)S(1)}, bf16[768,512]{1,0:T(8,128)(2,1)S(1)}, bf16[1024,2048]{1,0:T(8,128)(2,1)}) custom-call(s32[1]{0:T(128)} %bitcast.place_ref, s32[1024]{0:T(1024)S(1)} %bitcast.12, bf16[5120,128]{1,0:T(8,128)(2,1)S(1)} %bitcast.10, bf16[1024,2048]{1,0:T(8,128)(2,1)} %collective-permute-done.w_hbm), custom_call_target="tpu_custom_call", output_to_operand_aliasing={{2}: (3, {})} | custom-call | tf_op jit(solution)/shard_map/put/pallas_call | solution.py:137
  80.0 4.8 %collective-permute-start.2 = (bf16[768,512]{1,0:T(8,128)(2,1)S(1)}, bf16[768,512]{1,0:T(8,128)(2,1)S(1)}, u32[]{:S(2)}, u32[]{:S(2)}) collective-permute-start(bf16[768,512]{1,0:T(8,128)(2,1)S(1)} %get-tuple-element.20), channel_id=1, source_target_pairs={{0,1},{1,0},{2,3},{3,2},{4,5},{5,4},{6,7},{7,6},{8,9},{9,8},{10,11... | collective-permute-start | bytes 2359304 | tf_op jit(solution)/shard_map/ppermute | solution.py:382
  84.8 1.9 %collective-permute-done.2.theirs_ref = bf16[768,512]{1,0:T(8,128)(2,1)S(1)} collective-permute-done((bf16[768,512]{1,0:T(8,128)(2,1)S(1)}, bf16[768,512]{1,0:T(8,128)(2,1)S(1)}, u32[]{:S(2)}, u32[]{:S(2)}) %collective-permute-start.2) | collective-permute-done | bytes 786464 | tf_op jit(solution)/shard_map/ppermute | solution.py:382
  86.7 0.0 copy-done.1
  86.7 0.0 copy-done.4
  86.7 0.0 copy-done.3
  86.7 11.9 %layer.1 = (bf16[512,512]{1,0:T(8,128)(2,1)S(1)}, bf16[512,1024]{1,0:T(8,128)(2,1)S(1)}) custom-call(s32[1]{0:T(128)} %bitcast.place_ref, s32[1,8]{1,0:T(1,128)S(1)} %copy-done.4, bf16[768,512]{1,0:T(8,128)(2,1)S(1)} %get-tuple-element.19.mine_ref, bf16[768,512]{1,0:T(8,128)(2,1)S(1)} %collective-permute-done.2.theirs_ref, bf16[1024,2048]{1,0:T(8,128)(2,1)S(1)} %copy-done.3, ...), custom_call_target="tpu_custom_call" | custom-call | flops 7516192768 | bytes 12582912 | tf_op jit(solution)/shard_map/layer/pallas_call | solution.py:275
  98.6 0.5 collective-permute-start.3
  99.1 1.7 %keep.1.half_hbm = bf16[1024,512]{1,0:T(8,128)(2,1)} custom-call(s32[1]{0:T(128)} %bitcast.place_ref, bf16[512,1024]{1,0:T(8,128)(2,1)S(1)} %get-tuple-element.24.hidden_ref, bf16[768,512]{1,0:T(8,128)(2,1)S(1)} %get-tuple-element.19.mine_ref, bf16[512,1024]{1,0:T(8,128)(2,1)S(1)} %copy-done.1, bf16[512,1024]{1,0:T(8,128)(2,1)S(1)} %collective-permute-done.1.wo1_hbm), custom_call_target="tpu_custom_call" | custom-call | flops 536870912 | bytes 3145728 | tf_op jit(solution)/shard_map/keep/pallas_call | solution.py:326
  100.8 0.0 collective-permute-done.3.got_ref
  100.8 0.8 join.1
  (3 shorter events, 0.0 us)
Async XLA Ops:
  0.0 30.8 %collective-permute-start = (bf16[1024,2048]{1,0:T(8,128)(2,1)}, bf16[1024,2048]{1,0:T(8,128)(2,1)}, u32[]{:S(2)}, u32[]{:S(2)}) collective-permute-start(bf16[1024,2048]{1,0:T(8,128)(2,1)} %wq0_ref.1), channel_id=1, source_target_pairs={{0,1},{1,0},{2,3},{3,2},{4,5},{5,4},{6,7},{7,6},{8,9},{9,8},{10,11... | collective-permute-start | bytes 12582920 | tf_op jit(solution)/shard_map/ppermute | solution.py:374
  3.2 27.6 %collective-permute-start.1 = (bf16[512,1024]{1,0:T(8,128)(2,1)}, bf16[512,1024]{1,0:T(8,128)(2,1)S(1)}, u32[]{:S(2)}, u32[]{:S(2)}) collective-permute-start(bf16[512,1024]{1,0:T(8,128)(2,1)} %wo0_hbm.3), channel_id=1, source_target_pairs={{0,1},{1,0},{2,3},{3,2},{4,5},{5,4},{6,7},{7,6},{8,9},{9,8},{10,11... | collective-permute-start | bytes 3145736 | tf_op jit(solution)/shard_map/ppermute | solution.py:375
  6.2 71.2 %copy-start.2 = (s32[8,128]{1,0:T(8,128)S(1)}, s32[8,128]{1,0:T(8,128)}, u32[]{:S(2)}) copy-start(s32[8,128]{1,0:T(8,128)} %get-tuple-element.15) | copy-start | bytes 12292
  30.8 2.2 %copy-start = (bf16[4096,512]{1,0:T(8,128)(2,1)S(1)}, bf16[4096,512]{1,0:T(8,128)(2,1)}, u32[]{:S(2)}) copy-start(bf16[4096,512]{1,0:T(8,128)(2,1)} %table_ref.1) | copy-start | bytes 12582916
  38.1 48.6 %copy-start.1 = (bf16[512,1024]{1,0:T(8,128)(2,1)S(1)}, bf16[512,1024]{1,0:T(8,128)(2,1)}, u32[]{:S(2)}) copy-start(bf16[512,1024]{1,0:T(8,128)(2,1)} %wo0_hbm.3) | copy-start | bytes 3145732
  38.1 48.6 %copy-start.4 = (s32[1,8]{1,0:T(1,128)S(1)}, s32[1,8]{1,0:T(1,128)}, u32[]{:S(2)}) copy-start(s32[1,8]{1,0:T(1,128)} %lengths_ref.1) | copy-start | bytes 100
  38.1 39.2 %all-to-all-start.1 = ((bf16[128,40,128]{2,1,0:T(8,128)(2,1)}), bf16[128,40,128]{2,1,0:T(8,128)(2,1)S(1)}, u32[]{:S(2)}, u32[]{:S(2)}) async-start(bf16[128,40,128]{2,1,0:T(8,128)(2,1)} %bitcast.7), calls=%async_computation.1 | async-start | bytes 2621440 | tf_op jit(solution)/shard_map/all_to_all | solution.py:380
  77.3 9.4 %copy-start.3 = (bf16[1024,2048]{1,0:T(8,128)(2,1)S(1)}, bf16[1024,2048]{1,0:T(8,128)(2,1)}, u32[]{:S(2)}) copy-start(bf16[1024,2048]{1,0:T(8,128)(2,1)} %wq0_ref.1) | copy-start | bytes 12582916
  80.0 6.7 %collective-permute-start.2 = (bf16[768,512]{1,0:T(8,128)(2,1)S(1)}, bf16[768,512]{1,0:T(8,128)(2,1)S(1)}, u32[]{:S(2)}, u32[]{:S(2)}) collective-permute-start(bf16[768,512]{1,0:T(8,128)(2,1)S(1)} %get-tuple-element.20), channel_id=1, source_target_pairs={{0,1},{1,0},{2,3},{3,2},{4,5},{5,4},{6,7},{7,6},{8,9},{9,8},{10,11... | collective-permute-start | bytes 2359304 | tf_op jit(solution)/shard_map/ppermute | solution.py:382
  98.6 2.2 %collective-permute-start.3 = (bf16[512,512]{1,0:T(8,128)(2,1)S(1)}, bf16[512,512]{1,0:T(8,128)(2,1)S(1)}, u32[]{:S(2)}, u32[]{:S(2)}) collective-permute-start(bf16[512,512]{1,0:T(8,128)(2,1)S(1)} %get-tuple-element.23), channel_id=1, source_target_pairs={{0,1},{1,0},{2,3},{3,2},{4,5},{5,4},{6,7},{7,6},{8,9},{9,8},{10,11... | collective-permute-start | bytes 1572872 | tf_op jit(solution)/shard_map/ppermute | solution.py:384

commit v3 on v2

--- a/solution.py
+++ b/solution.py
@@ -19,32 +19,34 @@
 
 
 def route_kernel(owner_ref, row_ref, wanted_ref, dest_ref):
+    blocks = TOK // 128
     sub = lax.broadcasted_iota(jnp.int32, (128, 128), 0)
     lane = lax.broadcasted_iota(jnp.int32, (128, 128), 1)
     before = (sub < lane).astype(F32).astype(BF16)
+    hits = [(sub == owner_ref[b : b + 1, :]).astype(F32) for b in range(blocks)]
+    ranks = jnp.dot(
+        jnp.concatenate(hits, axis=0).astype(BF16), before, preferred_element_type=F32
+    )
     count = jnp.zeros((128, 1), F32)
-    high = jnp.zeros((128, 128), F32)
-    low = jnp.zeros((128, 128), F32)
-    for b in range(TOK // 128):
-        owner = owner_ref[b : b + 1, :]
+    kind = lax.broadcasted_iota(jnp.int32, (32, 128), 0)
+    values = []
+    for b in range(blocks):
+        rank = ranks[b * 128 : (b + 1) * 128] + count
+        slot = jnp.sum(hits[b] * rank, axis=0, keepdims=True).astype(jnp.int32)
+        count = count + jnp.sum(hits[b], axis=1, keepdims=True)
+        dest_ref[b : b + 1, :] = owner_ref[b : b + 1, :] * CAP + slot
         row = row_ref[b : b + 1, :]
-        hit = (sub == owner).astype(F32)
-        hit16 = hit.astype(BF16)
-        rank = jnp.dot(hit16, before, preferred_element_type=F32) + count
-        slot = jnp.sum(hit * rank, axis=0, keepdims=True).astype(jnp.int32)
-        count = count + jnp.sum(hit, axis=1, keepdims=True)
-        dest_ref[b : b + 1, :] = owner * CAP + slot
-        here = sub == slot
         spot = ((row >> 3) << 5) + (row & 7)
-        top = (spot >> 6).astype(F32)
-        rest = (spot & 63).astype(F32)
-        high += lax.dot_general(
-            hit16, jnp.where(here, top, 0.0).astype(BF16), NT, preferred_element_type=F32
-        )
-        low += lax.dot_general(
-            hit16, jnp.where(here, rest, 0.0).astype(BF16), NT, preferred_element_type=F32
-        )
-    wanted_ref[...] = (high * 64.0 + low).astype(jnp.int32)
+        part = jnp.where(kind < 16, spot >> 6, spot & 63).astype(F32)
+        values.append(jnp.where((kind & 15) == slot, part, 0.0))
+    both = lax.dot_general(
+        jnp.concatenate(hits, axis=1).astype(BF16),
+        jnp.concatenate(values, axis=1).astype(BF16),
+        NT,
+        preferred_element_type=F32,
+    )
+    wanted_ref[...] = jnp.zeros((128, 128), jnp.int32)
+    wanted_ref[:, :16] = (both[:, :16] * 64.0 + both[:, 16:]).astype(jnp.int32)
 
 
 def route(owner, row):
@@ -54,11 +56,29 @@
             jax.ShapeDtypeStruct((128, 128), jnp.int32),
             jax.ShapeDtypeStruct((8, 128), jnp.int32),
         ),
+        cost_estimate=pl.CostEstimate(
+            flops=1 << 32, bytes_accessed=1 << 20, transcendentals=0
+        ),
         name="route",
     )(owner.reshape(8, 128), row.reshape(8, 128))
 
 
-def fetch_kernel(asked_ref, table_ref, out_ref, tall_ref, wide_ref):
+PIECES = 8
+
+
+def fetch_kernel(asked_ref, table_hbm, out_ref, table_ref, tall_ref, wide_ref, sems):
+    rows = 4096 // PIECES
+    copies = [
+        pltpu.make_async_copy(
+            table_hbm.at[pl.ds(i * rows, rows), :],
+            table_ref.at[pl.ds(i * rows, rows), :],
+            sems.at[i],
+        )
+        for i in range(PIECES)
+    ]
+    for cp in copies:
+        cp.start()
+
     def widen(j, _):
         at = pl.ds(pl.multiple_of(j * 16, 16), 16)
         for k in range(4):
@@ -67,7 +87,9 @@
             tall_ref[pl.ds(pl.multiple_of(j * 64 + 32 + k * 8, 8), 8), :] = v[8:]
         return 0
 
-    lax.fori_loop(0, 4096 // 16, widen, 0, unroll=4)
+    for i in range(PIECES):
+        copies[i].wait()
+        lax.fori_loop(i * rows // 16, (i + 1) * rows // 16, widen, 0, unroll=4)
 
     def body(g, _):
         for s in range(CAP):
@@ -75,8 +97,8 @@
             wide_ref[pl.ds(g * 40 + 4 * s, 4), :] = tall_ref[pl.ds(at, 4, stride=8), :]
         return 0
 
-    lax.fori_loop(0, 128, body, 0, unroll=2)
-    out_ref[...] = wide_ref[...].astype(BF16)
+    lax.fori_loop(0, 128, body, 0, unroll=8)
+    out_ref[...] = wide_ref[: 128 * 40, :].astype(BF16)
 
 
 def fetch(asked, table):
@@ -85,72 +107,71 @@
         out_shape=jax.ShapeDtypeStruct((128 * 40, 128), BF16),
         in_specs=[
             pl.BlockSpec(memory_space=pltpu.SMEM),
-            pl.BlockSpec(memory_space=pltpu.VMEM),
+            pl.BlockSpec(memory_space=pltpu.HBM),
         ],
         out_specs=pl.BlockSpec(memory_space=pltpu.VMEM),
         scratch_shapes=[
-            pltpu.VMEM((4096 * 4, 128), F32),
-            pltpu.VMEM((128 * 40, 128), F32),
-        ],
-        compiler_params=pltpu.CompilerParams(vmem_limit_bytes=18 << 20),
+            pltpu.VMEM((4096, HALF), BF16),
+            pltpu.VMEM((4096 * 4 + 32, 128), F32),
+            pltpu.VMEM((128 * 40 + 8, 128), F32),
+            pltpu.SemaphoreType.DMA((PIECES,)),
+        ],
+        compiler_params=pltpu.CompilerParams(vmem_limit_bytes=60 << 20),
         name="fetch",
     )(asked, table)
 
 
-def place_kernel(
-    place_ref, dest_ref, arrived_ref, w_hbm, mine_ref, send_ref, held_hbm, wide_ref, emb_ref
-):
-    wide_ref[...] = arrived_ref[...].astype(F32)
+def place_kernel(target_ref, dest_ref, arrived_ref, *refs):
+    out_ref, wide_ref, emb_ref = refs[-4], refs[-2], refs[-1]
+    wide_ref[: 128 * 40, :] = arrived_ref[...].astype(F32)
+    base = target_ref[0] * HALF - MAX_LEN
 
     def body(j, _):
+        token = base + j * 8
+        token = jnp.where(token < 0, 0, token)
         for r in range(8):
-            at = dest_ref[j * 8 + r]
-            emb_ref[pl.ds(MAX_LEN * 4 + j * 32 + r, 4, stride=8), :] = wide_ref[
+            at = dest_ref[token + r]
+            emb_ref[pl.ds(j * 32 + r, 4, stride=8), :] = wide_ref[
                 pl.ds(pl.multiple_of(at * 4, 4), 4), :
             ]
         return 0
 
-    lax.fori_loop(0, TOK // 8, body, 0, unroll=2)
-    emb_ref[: MAX_LEN * 4, :] = jnp.zeros((MAX_LEN * 4, 128), F32)
-    c = place_ref[0]
-
-    def window(out_ref, base):
-        def body(m, _):
-            rows = pl.ds(pl.multiple_of(m * 16, 16), 16)
-            for k in range(4):
-                lo = emb_ref[pl.ds(pl.multiple_of(base + m * 64 + k * 8, 8), 8), :]
-                hi = emb_ref[pl.ds(pl.multiple_of(base + m * 64 + 32 + k * 8, 8), 8), :]
-                out_ref[rows, k * 128 : (k + 1) * 128] = jnp.concatenate(
-                    [lo, hi], axis=0
-                ).astype(BF16)
-            return 0
-
-        lax.fori_loop(0, WIN // 16, body, 0, unroll=4)
-
-    window(send_ref, pl.multiple_of((1 - c) * HALF * 4, HALF * 4))
-    window(mine_ref, pl.multiple_of(c * HALF * 4, HALF * 4))
-
-
-def put(place, dest, arrived, w):
+    lax.fori_loop(0, WIN // 8, body, 0, unroll=2)
+
+    def pack(m, _):
+        rows = pl.ds(pl.multiple_of(m * 16, 16), 16)
+        for k in range(4):
+            lo = emb_ref[pl.ds(pl.multiple_of(m * 64 + k * 8, 8), 8), :]
+            hi = emb_ref[pl.ds(pl.multiple_of(m * 64 + 32 + k * 8, 8), 8), :]
+            out_ref[rows, k * 128 : (k + 1) * 128] = jnp.concatenate([lo, hi], axis=0).astype(BF16)
+        return 0
+
+    lax.fori_loop(0, WIN // 16, pack, 0, unroll=4)
+
+
+def put(target, dest, arrived, w):
     vmem = pl.BlockSpec(memory_space=pltpu.VMEM)
     smem = pl.BlockSpec(memory_space=pltpu.SMEM)
+    hbm = pl.BlockSpec(memory_space=pltpu.HBM)
     return pl.pallas_call(
         place_kernel,
         out_shape=(
             jax.ShapeDtypeStruct((WIN, HALF), BF16),
-            jax.ShapeDtypeStruct((WIN, HALF), BF16),
             jax.ShapeDtypeStruct((D, 4 * HALF), BF16),
         ),
-        in_specs=[smem, smem, vmem, pl.BlockSpec(memory_space=pltpu.HBM)],
-        out_specs=(vmem, vmem, pl.BlockSpec(memory_space=pltpu.HBM)),
-        input_output_aliases={3: 2},
+        in_specs=[smem, smem, vmem, hbm],
+        out_specs=(vmem, hbm),
+        input_output_aliases={3: 1},
         scratch_shapes=[
-            pltpu.VMEM((128 * 40, 128), F32),
-            pltpu.VMEM(((TOK + MAX_LEN) * 4, 128), F32),
+            pltpu.VMEM((128 * 40 + 8, 128), F32),
+            pltpu.VMEM((WIN * 4 + 32, 128), F32),
         ],
         compiler_params=pltpu.CompilerParams(vmem_limit_bytes=12 << 20),
+        cost_estimate=pl.CostEstimate(
+            flops=1 << 20, bytes_accessed=6 << 20, transcendentals=0
+        ),
         name="put",
-    )(place, dest, arrived, w)
+    )(target, dest, arrived, w)
 
 
 def silu(x):
@@ -378,8 +399,10 @@
     asked, wq1, wo1 = lax.optimization_barrier((asked, wq1, wo1))
     fetched = fetch(asked[:, 0, :], table)
     arrived = lax.all_to_all(fetched.reshape(128, 4 * CAP, 128), "dp", 0, 0, tiled=True)
-    mine, send, held = put(place, dest, arrived.reshape(128 * 4 * CAP, 128), wq1)
+    arrived = arrived.reshape(128 * 4 * CAP, 128)
+    send, held = put(1 - place, dest, arrived, wq1)
     theirs = lax.ppermute(send, "col", swap)
+    mine, held = put(place, dest, arrived, held)
     out, hidden = layer(place, seq_lengths, mine, theirs, w_qkvu, held, w_out, wo1)
     got = lax.ppermute(out, "col", swap)
     half = keep(place, hidden, mine, w_out, wo1)

time: 102 us -> 100 us (0.980)
  local copies, waits for them, and re-layouts: 2.2 us -> 0.01 us
  waiting for transfers between devices: 34.8 us -> 33 us
  Pallas kernels: 25.2 us -> 26.9 us
    unnamed x10 -> x8, local copies, waits for them, and re-layouts: 2.2 us -> 0.01 us
    ppermute x1, waiting for transfers between devices: 1.91 us -> 0.01 us  [local(): theirs = lax.ppermute(send, 'col', swap)]
    pallas_call x1 -> x2, Pallas kernels: 2.67 us -> 4.24 us  [put(): pl.pallas_call(place_kernel, out_shape=(jax.ShapeDtypeStruct((WIN, HALF),...]
    pallas_call x1, Pallas kernels: 5.11 us -> 6.49 us  [fetch(): pl.pallas_call(fetch_kernel, out_shape=jax.ShapeDtypeStruct((128 * 40, 12...]
    pallas_call x1, Pallas kernels: 2.96 us -> 1.85 us  [route(): pl.pallas_call(route_kernel, out_shape=(jax.ShapeDtypeStruct((128, 128),...]
  transfers between devices with their start and end apart: 5 -> 5, of which waited for: 2 -> 2; matrix products, arithmetic and copies ran while one was open for 0% -> 0% of each run, Pallas kernels for 5% -> 6%
where the time goes in v3:
time: 100 us; the launch traced here: 99.7 us
  waiting for transfers between devices  33 us (33%)
  Pallas kernels  26.9 us (27%)
  blocking collectives  25.2 us (25%)
  starting transfers between devices  14.3 us (14%)
    all_to_all x1, waiting for transfers between devices, local(): lax.all_to_all(fetched.reshape(128, 4 * CAP, 128), 'dp', 0, 0, tiled=True)  32.9 us
    all_to_all x1, blocking collectives, local(): asked = lax.all_to_all(wanted[:, None, :], 'dp', 0, 0, tiled=True)  25.2 us
    pallas_call x1, Pallas kernels, layer(): pl.pallas_call(layer_kernel, out_shape=(jax.ShapeDtypeStruct((HALF, HALF)...  11.8 us
    pallas_call x1, Pallas kernels, fetch(): pl.pallas_call(fetch_kernel, out_shape=jax.ShapeDtypeStruct((128 * 40, 12...  6.49 us
    all_to_all x1, starting transfers between devices, local(): lax.all_to_all(fetched.reshape(128, 4 * CAP, 128), 'dp', 0, 0, tiled=True)  6.21 us
    ppermute x1, starting transfers between devices, local(): theirs = lax.ppermute(send, 'col', swap)  4.68 us
    pallas_call x2, Pallas kernels, put(): pl.pallas_call(place_kernel, out_shape=(jax.ShapeDtypeStruct((WIN, HALF),...  4.24 us
    ppermute x1, starting transfers between devices, local(): wq1 = lax.ppermute(w_qkvu, 'col', swap)  3.2 us
  transfers between devices with their start and end apart: 5, of which 2 were waited for; matrix products, arithmetic and copies ran while one was open for 0% of the time, Pallas kernels for 6%

profile of v3, /device:TPU:1, one launch (start us, length us, event | category | flops | bytes accessed | tf_op | source)
XLA Modules:
  0.0 99.7 jit_solution(12252259190841144555)
XLA Ops:
  0.0 3.2 %collective-permute-start = (bf16[1024,2048]{1,0:T(8,128)(2,1)}, bf16[1024,2048]{1,0:T(8,128)(2,1)}, u32[]{:S(2)}, u32[]{:S(2)}) collective-permute-start(bf16[1024,2048]{1,0:T(8,128)(2,1)} %wq0_ref.1), channel_id=1, source_target_pairs={{0,1},{1,0},{2,3},{3,2},{4,5},{5,4},{6,7},{7,6},{8,9},{9,8},{10,11... | collective-permute-start | bytes 12582920 | tf_op jit(solution)/shard_map/ppermute | solution.py:395
  3.2 0.0 collective-permute-start.1
  3.2 1.8 %route.1 = (s32[128,128]{1,0:T(8,128)}, s32[8,128]{1,0:T(8,128)}) custom-call(s32[8,128]{1,0:T(8,128)} %bitcast.17, s32[8,128]{1,0:T(8,128)} %bitcast.18), custom_call_target="tpu_custom_call" | custom-call | flops 4294967296 | bytes 1048576 | tf_op jit(solution)/shard_map/route/pallas_call | solution.py:53
  5.1 0.0 copy-start.1
  5.1 25.2 %all_to_all.10 = s32[128,1,128]{2,1,0:T(1,128)} all-to-all(s32[128,1,128]{2,1,0:T(1,128)} %bitcast.16), channel_id=1, replica_groups=mesh['dp'=128,'col'=2] {'dp'}, dimensions={0} | all-to-all | bytes 131072 | tf_op jit(solution)/shard_map/all_to_all | solution.py:394
  30.2 0.0 collective-permute-done.1.wo1_hbm
  30.2 0.0 collective-permute-done.refs_0_
  30.2 6.5 %fetch.1 = bf16[5120,128]{1,0:T(8,128)(2,1)} custom-call(s32[128,128]{1,0:T(8,128)} %bitcast.15, bf16[4096,512]{1,0:T(8,128)(2,1)} %table_hbm.1), custom_call_target="tpu_custom_call" | custom-call | tf_op jit(solution)/shard_map/fetch/pallas_call | solution.py:105
  36.7 6.2 %all-to-all-start.1 = ((bf16[128,40,128]{2,1,0:T(8,128)(2,1)}), bf16[128,40,128]{2,1,0:T(8,128)(2,1)S(1)}, u32[]{:S(2)}, u32[]{:S(2)}) async-start(bf16[128,40,128]{2,1,0:T(8,128)(2,1)} %bitcast.14), calls=%async_computation.1 | async-start | bytes 2621440 | tf_op jit(solution)/shard_map/all_to_all | solution.py:401
  42.9 32.9 %all-to-all-done.1 = bf16[128,40,128]{2,1,0:T(8,128)(2,1)S(1)} async-done(((bf16[128,40,128]{2,1,0:T(8,128)(2,1)}), bf16[128,40,128]{2,1,0:T(8,128)(2,1)S(1)}, u32[]{:S(2)}, u32[]{:S(2)}) %all-to-all-start.1) | async-done | bytes 1310752 | tf_op jit(solution)/shard_map/all_to_all | solution.py:401
  75.9 0.0 copy-done.1
  75.9 0.0 copy-start
  75.9 2.1 %put.2 = (bf16[768,512]{1,0:T(8,128)(2,1)S(1)}, bf16[1024,2048]{1,0:T(8,128)(2,1)}) custom-call(s32[1]{0:T(128)S(6)} %sub.3.target_ref, s32[1024]{0:T(1024)S(1)} %bitcast.12, bf16[5120,128]{1,0:T(8,128)(2,1)S(1)} %bitcast.10, bf16[1024,2048]{1,0:T(8,128)(2,1)} %collective-permute-done.refs_0_), custom_call_target="tpu_custom_call", output_to_operand_aliasing={{1}: (3, {})} | custom-call | flops 1048576 | bytes 6291456 | tf_op jit(solution)/shard_map/put/pallas_call | solution.py:156
  78.0 4.7 %collective-permute-start.2 = (bf16[768,512]{1,0:T(8,128)(2,1)S(1)}, bf16[768,512]{1,0:T(8,128)(2,1)S(1)}, u32[]{:S(2)}, u32[]{:S(2)}) collective-permute-start(bf16[768,512]{1,0:T(8,128)(2,1)S(1)} %get-tuple-element.22), channel_id=1, source_target_pairs={{0,1},{1,0},{2,3},{3,2},{4,5},{5,4},{6,7},{7,6},{8,9},{9,8},{10,11... | collective-permute-start | bytes 2359304 | tf_op jit(solution)/shard_map/ppermute | solution.py:404
  82.7 2.1 %put.3 = (bf16[768,512]{1,0:T(8,128)(2,1)S(1)}, bf16[1024,2048]{1,0:T(8,128)(2,1)}) custom-call(s32[1]{0:T(128)} %bitcast.target_ref.place_ref, s32[1024]{0:T(1024)S(1)} %bitcast.13, bf16[5120,128]{1,0:T(8,128)(2,1)S(1)} %bitcast.11, bf16[1024,2048]{1,0:T(8,128)(2,1)} %get-tuple-element.20.refs_0_), custom_call_target="tpu_custom_call", output_to_operand_aliasing={{1}: (3, {})} | custom-call | flops 1048576 | bytes 6291456 | tf_op jit(solution)/shard_map/put/pallas_call | solution.py:156
  84.8 0.0 collective-permute-done.2.theirs_ref
  84.8 0.0 copy-done
  84.8 0.0 copy-done.2
  84.8 0.0 copy-done.3
  84.9 11.8 %layer.1 = (bf16[512,512]{1,0:T(8,128)(2,1)S(1)}, bf16[512,1024]{1,0:T(8,128)(2,1)S(1)}) custom-call(s32[1]{0:T(128)} %bitcast.target_ref.place_ref, s32[1,8]{1,0:T(1,128)S(1)} %copy-done.3, bf16[768,512]{1,0:T(8,128)(2,1)S(1)} %get-tuple-element.21.mine_ref, bf16[768,512]{1,0:T(8,128)(2,1)S(1)} %collective-permute-done.2.theirs_ref, ...), custom_call_target="tpu_custom_call" | custom-call | flops 7516192768 | bytes 12582912 | tf_op jit(solution)/shard_map/layer/pallas_call | solution.py:296
  96.7 0.2 collective-permute-start.3
  96.9 1.7 %keep.1.half_hbm = bf16[1024,512]{1,0:T(8,128)(2,1)} custom-call(s32[1]{0:T(128)} %bitcast.target_ref.place_ref, bf16[512,1024]{1,0:T(8,128)(2,1)S(1)} %get-tuple-element.26.hidden_ref, bf16[768,512]{1,0:T(8,128)(2,1)S(1)} %get-tuple-element.21.mine_ref, bf16[512,1024]{1,0:T(8,128)(2,1)S(1)} %copy-done, bf16[512,1024]{1,0:T(8,128)(2,1)S(1)} %collective-permute-done.1.wo1_hbm), custom_call_target="tpu_custom_call" | custom-call | flops 536870912 | bytes 3145728 | tf_op jit(solution)/shard_map/keep/pallas_call | solution.py:347
  98.6 0.1 collective-permute-done.3.got_ref
  98.7 0.8 join.1
  (2 shorter events, 0.0 us)
Async XLA Ops:
  0.0 30.2 %collective-permute-start = (bf16[1024,2048]{1,0:T(8,128)(2,1)}, bf16[1024,2048]{1,0:T(8,128)(2,1)}, u32[]{:S(2)}, u32[]{:S(2)}) collective-permute-start(bf16[1024,2048]{1,0:T(8,128)(2,1)} %wq0_ref.1), channel_id=1, source_target_pairs={{0,1},{1,0},{2,3},{3,2},{4,5},{5,4},{6,7},{7,6},{8,9},{9,8},{10,11... | collective-permute-start | bytes 12582920 | tf_op jit(solution)/shard_map/ppermute | solution.py:395
  3.2 27.0 %collective-permute-start.1 = (bf16[512,1024]{1,0:T(8,128)(2,1)}, bf16[512,1024]{1,0:T(8,128)(2,1)S(1)}, u32[]{:S(2)}, u32[]{:S(2)}) collective-permute-start(bf16[512,1024]{1,0:T(8,128)(2,1)} %wo0_hbm.3), channel_id=1, source_target_pairs={{0,1},{1,0},{2,3},{3,2},{4,5},{5,4},{6,7},{7,6},{8,9},{9,8},{10,11... | collective-permute-start | bytes 3145736 | tf_op jit(solution)/shard_map/ppermute | solution.py:396
  5.1 70.8 %copy-start.1 = (s32[8,128]{1,0:T(8,128)S(1)}, s32[8,128]{1,0:T(8,128)}, u32[]{:S(2)}) copy-start(s32[8,128]{1,0:T(8,128)} %get-tuple-element.16) | copy-start | bytes 12292
  36.7 39.2 %all-to-all-start.1 = ((bf16[128,40,128]{2,1,0:T(8,128)(2,1)}), bf16[128,40,128]{2,1,0:T(8,128)(2,1)S(1)}, u32[]{:S(2)}, u32[]{:S(2)}) async-start(bf16[128,40,128]{2,1,0:T(8,128)(2,1)} %bitcast.14), calls=%async_computation.1 | async-start | bytes 2621440 | tf_op jit(solution)/shard_map/all_to_all | solution.py:401
  75.9 9.0 %copy-start = (bf16[512,1024]{1,0:T(8,128)(2,1)S(1)}, bf16[512,1024]{1,0:T(8,128)(2,1)}, u32[]{:S(2)}) copy-start(bf16[512,1024]{1,0:T(8,128)(2,1)} %wo0_hbm.3) | copy-start | bytes 3145732
  75.9 9.0 %copy-start.2 = (bf16[1024,2048]{1,0:T(8,128)(2,1)S(1)}, bf16[1024,2048]{1,0:T(8,128)(2,1)}, u32[]{:S(2)}) copy-start(bf16[1024,2048]{1,0:T(8,128)(2,1)} %wq0_ref.1) | copy-start | bytes 12582916
  75.9 9.0 %copy-start.3 = (s32[1,8]{1,0:T(1,128)S(1)}, s32[1,8]{1,0:T(1,128)}, u32[]{:S(2)}) copy-start(s32[1,8]{1,0:T(1,128)} %lengths_ref.1) | copy-start | bytes 100
  78.0 6.8 %collective-permute-start.2 = (bf16[768,512]{1,0:T(8,128)(2,1)S(1)}, bf16[768,512]{1,0:T(8,128)(2,1)S(1)}, u32[]{:S(2)}, u32[]{:S(2)}) collective-permute-start(bf16[768,512]{1,0:T(8,128)(2,1)S(1)} %get-tuple-element.22), channel_id=1, source_target_pairs={{0,1},{1,0},{2,3},{3,2},{4,5},{5,4},{6,7},{7,6},{8,9},{9,8},{10,11... | collective-permute-start | bytes 2359304 | tf_op jit(solution)/shard_map/ppermute | solution.py:404
  96.7 2.0 %collective-permute-start.3 = (bf16[512,512]{1,0:T(8,128)(2,1)S(1)}, bf16[512,512]{1,0:T(8,128)(2,1)S(1)}, u32[]{:S(2)}, u32[]{:S(2)}) collective-permute-start(bf16[512,512]{1,0:T(8,128)(2,1)S(1)} %get-tuple-element.25), channel_id=1, source_target_pairs={{0,1},{1,0},{2,3},{3,2},{4,5},{5,4},{6,7},{7,6},{8,9},{9,8},{10,11... | collective-permute-start | bytes 1572872 | tf_op jit(solution)/shard_map/ppermute | solution.py:407

commit v4 on v3

--- a/solution.py
+++ b/solution.py
@@ -66,7 +66,9 @@
 PIECES = 8
 
 
-def fetch_kernel(asked_ref, table_hbm, out_ref, table_ref, tall_ref, wide_ref, sems):
+def fetch_kernel(
+    asked_hbm, table_hbm, out_ref, asked_ref, table_ref, tall_ref, wide_ref, sems
+):
     rows = 4096 // PIECES
     copies = [
         pltpu.make_async_copy(
@@ -78,6 +80,8 @@
     ]
     for cp in copies:
         cp.start()
+    listing = pltpu.make_async_copy(asked_hbm, asked_ref, sems.at[PIECES])
+    listing.start()
 
     def widen(j, _):
         at = pl.ds(pl.multiple_of(j * 16, 16), 16)
@@ -89,7 +93,9 @@
 
     for i in range(PIECES):
         copies[i].wait()
-        lax.fori_loop(i * rows // 16, (i + 1) * rows // 16, widen, 0, unroll=4)
+        lax.fori_loop(i * rows // 16, (i + 1) * rows // 16, widen, 0, unroll=8)
+
+    listing.wait()
 
     def body(g, _):
         for s in range(CAP):
@@ -97,7 +103,7 @@
             wide_ref[pl.ds(g * 40 + 4 * s, 4), :] = tall_ref[pl.ds(at, 4, stride=8), :]
         return 0
 
-    lax.fori_loop(0, 128, body, 0, unroll=8)
+    lax.fori_loop(0, 128, body, 0, unroll=16)
     out_ref[...] = wide_ref[: 128 * 40, :].astype(BF16)
 
 
@@ -106,15 +112,16 @@
         fetch_kernel,
         out_shape=jax.ShapeDtypeStruct((128 * 40, 128), BF16),
         in_specs=[
-            pl.BlockSpec(memory_space=pltpu.SMEM),
+            pl.BlockSpec(memory_space=pltpu.HBM),
             pl.BlockSpec(memory_space=pltpu.HBM),
         ],
         out_specs=pl.BlockSpec(memory_space=pltpu.VMEM),
         scratch_shapes=[
+            pltpu.SMEM((128, 128), jnp.int32),
             pltpu.VMEM((4096, HALF), BF16),
             pltpu.VMEM((4096 * 4 + 32, 128), F32),
             pltpu.VMEM((128 * 40 + 8, 128), F32),
-            pltpu.SemaphoreType.DMA((PIECES,)),
+            pltpu.SemaphoreType.DMA((PIECES + 1,)),
         ],
         compiler_params=pltpu.CompilerParams(vmem_limit_bytes=60 << 20),
         name="fetch",
@@ -136,7 +143,7 @@
             ]
         return 0
 
-    lax.fori_loop(0, WIN // 8, body, 0, unroll=2)
+    lax.fori_loop(0, WIN // 8, body, 0, unroll=8)
 
     def pack(m, _):
         rows = pl.ds(pl.multiple_of(m * 16, 16), 16)
@@ -146,7 +153,7 @@
             out_ref[rows, k * 128 : (k + 1) * 128] = jnp.concatenate([lo, hi], axis=0).astype(BF16)
         return 0
 
-    lax.fori_loop(0, WIN // 16, pack, 0, unroll=4)
+    lax.fori_loop(0, WIN // 16, pack, 0, unroll=8)
 
 
 def put(target, dest, arrived, w):

time: 100 us -> 97.9 us (0.979)
  Pallas kernels: 26.9 us -> 24.8 us
    pallas_call x1, Pallas kernels: 6.49 us -> 4.71 us  [fetch(): pl.pallas_call(fetch_kernel, out_shape=jax.ShapeDtypeStruct((128 * 40, 12...]
  transfers between devices with their start and end apart: 5 -> 5, of which waited for: 2 -> 1; matrix products, arithmetic and copies ran while one was open for 0% -> 0% of each run, Pallas kernels for 6% -> 6%
where the time goes in v4:
time: 97.9 us; the launch traced here: 97.6 us
  waiting for transfers between devices  32.9 us (34%)
  blocking collectives  25.2 us (26%)
  Pallas kernels  24.8 us (25%)
  starting transfers between devices  14.4 us (15%)
    all_to_all x1, waiting for transfers between devices, local(): lax.all_to_all(fetched.reshape(128, 4 * CAP, 128), 'dp', 0, 0, tiled=True)  32.9 us
    all_to_all x1, blocking collectives, local(): asked = lax.all_to_all(wanted[:, None, :], 'dp', 0, 0, tiled=True)  25.2 us
    pallas_call x1, Pallas kernels, layer(): pl.pallas_call(layer_kernel, out_shape=(jax.ShapeDtypeStruct((HALF, HALF)...  11.8 us
    all_to_all x1, starting transfers between devices, local(): lax.all_to_all(fetched.reshape(128, 4 * CAP, 128), 'dp', 0, 0, tiled=True)  6.21 us
    pallas_call x1, Pallas kernels, fetch(): pl.pallas_call(fetch_kernel, out_shape=jax.ShapeDtypeStruct((128 * 40, 12...  4.71 us
    ppermute x1, starting transfers between devices, local(): theirs = lax.ppermute(send, 'col', swap)  4.68 us
    pallas_call x2, Pallas kernels, put(): pl.pallas_call(place_kernel, out_shape=(jax.ShapeDtypeStruct((WIN, HALF),...  3.91 us
    ppermute x1, starting transfers between devices, local(): wq1 = lax.ppermute(w_qkvu, 'col', swap)  3.2 us
  transfers between devices with their start and end apart: 5, of which 1 were waited for; matrix products, arithmetic and copies ran while one was open for 0% of the time, Pallas kernels for 6%

profile of v4, /device:TPU:1, one launch (start us, length us, event | category | flops | bytes accessed | tf_op | source)
XLA Modules:
  0.0 97.6 jit_solution(13113293496548714780)
XLA Ops:
  0.0 3.2 %collective-permute-start = (bf16[1024,2048]{1,0:T(8,128)(2,1)}, bf16[1024,2048]{1,0:T(8,128)(2,1)}, u32[]{:S(2)}, u32[]{:S(2)}) collective-permute-start(bf16[1024,2048]{1,0:T(8,128)(2,1)} %wq0_ref.1), channel_id=1, source_target_pairs={{0,1},{1,0},{2,3},{3,2},{4,5},{5,4},{6,7},{7,6},{8,9},{9,8},{10,11... | collective-permute-start | bytes 12582920 | tf_op jit(solution)/shard_map/ppermute | solution.py:402
  3.2 0.0 collective-permute-start.1
  3.2 1.8 %route.1 = (s32[128,128]{1,0:T(8,128)}, s32[8,128]{1,0:T(8,128)}) custom-call(s32[8,128]{1,0:T(8,128)} %bitcast.17, s32[8,128]{1,0:T(8,128)} %bitcast.18), custom_call_target="tpu_custom_call" | custom-call | flops 4294967296 | bytes 1048576 | tf_op jit(solution)/shard_map/route/pallas_call | solution.py:53
  5.1 0.0 copy-start.1
  5.1 25.2 %all_to_all.10 = s32[128,1,128]{2,1,0:T(1,128)} all-to-all(s32[128,1,128]{2,1,0:T(1,128)} %bitcast.16), channel_id=1, replica_groups=mesh['dp'=128,'col'=2] {'dp'}, dimensions={0} | all-to-all | bytes 131072 | tf_op jit(solution)/shard_map/all_to_all | solution.py:401
  30.2 0.0 collective-permute-done.1.wo1_hbm
  30.2 0.0 collective-permute-done.refs_0_
  30.2 4.7 %fetch.1 = bf16[5120,128]{1,0:T(8,128)(2,1)} custom-call(s32[128,128]{1,0:T(8,128)} %bitcast.15, bf16[4096,512]{1,0:T(8,128)(2,1)} %table_hbm.1), custom_call_target="tpu_custom_call" | custom-call | tf_op jit(solution)/shard_map/fetch/pallas_call | solution.py:111
  34.9 6.2 %all-to-all-start.1 = ((bf16[128,40,128]{2,1,0:T(8,128)(2,1)}), bf16[128,40,128]{2,1,0:T(8,128)(2,1)S(1)}, u32[]{:S(2)}, u32[]{:S(2)}) async-start(bf16[128,40,128]{2,1,0:T(8,128)(2,1)} %bitcast.14), calls=%async_computation.1 | async-start | bytes 2621440 | tf_op jit(solution)/shard_map/all_to_all | solution.py:408
  41.2 32.9 %all-to-all-done.1 = bf16[128,40,128]{2,1,0:T(8,128)(2,1)S(1)} async-done(((bf16[128,40,128]{2,1,0:T(8,128)(2,1)}), bf16[128,40,128]{2,1,0:T(8,128)(2,1)S(1)}, u32[]{:S(2)}, u32[]{:S(2)}) %all-to-all-start.1) | async-done | bytes 1310752 | tf_op jit(solution)/shard_map/all_to_all | solution.py:408
  74.1 0.0 copy-done.1
  74.1 0.0 copy-start
  74.1 2.0 %put.2 = (bf16[768,512]{1,0:T(8,128)(2,1)S(1)}, bf16[1024,2048]{1,0:T(8,128)(2,1)}) custom-call(s32[1]{0:T(128)S(6)} %sub.3.target_ref, s32[1024]{0:T(1024)S(1)} %bitcast.12, bf16[5120,128]{1,0:T(8,128)(2,1)S(1)} %bitcast.10, bf16[1024,2048]{1,0:T(8,128)(2,1)} %collective-permute-done.refs_0_), custom_call_target="tpu_custom_call", output_to_operand_aliasing={{1}: (3, {})} | custom-call | flops 1048576 | bytes 6291456 | tf_op jit(solution)/shard_map/put/pallas_call | solution.py:163
  76.1 4.7 %collective-permute-start.2 = (bf16[768,512]{1,0:T(8,128)(2,1)S(1)}, bf16[768,512]{1,0:T(8,128)(2,1)S(1)}, u32[]{:S(2)}, u32[]{:S(2)}) collective-permute-start(bf16[768,512]{1,0:T(8,128)(2,1)S(1)} %get-tuple-element.22), channel_id=1, source_target_pairs={{0,1},{1,0},{2,3},{3,2},{4,5},{5,4},{6,7},{7,6},{8,9},{9,8},{10,11... | collective-permute-start | bytes 2359304 | tf_op jit(solution)/shard_map/ppermute | solution.py:411
  80.7 2.0 %put.3 = (bf16[768,512]{1,0:T(8,128)(2,1)S(1)}, bf16[1024,2048]{1,0:T(8,128)(2,1)}) custom-call(s32[1]{0:T(128)} %bitcast.target_ref.place_ref, s32[1024]{0:T(1024)S(1)} %bitcast.13, bf16[5120,128]{1,0:T(8,128)(2,1)S(1)} %bitcast.11, bf16[1024,2048]{1,0:T(8,128)(2,1)} %get-tuple-element.20.refs_0_), custom_call_target="tpu_custom_call", output_to_operand_aliasing={{1}: (3, {})} | custom-call | flops 1048576 | bytes 6291456 | tf_op jit(solution)/shard_map/put/pallas_call | solution.py:163
  82.7 0.0 collective-permute-done.2.theirs_ref
  82.7 0.0 copy-done
  82.7 0.0 copy-done.2
  82.7 0.0 copy-done.3
  82.7 11.8 %layer.1 = (bf16[512,512]{1,0:T(8,128)(2,1)S(1)}, bf16[512,1024]{1,0:T(8,128)(2,1)S(1)}) custom-call(s32[1]{0:T(128)} %bitcast.target_ref.place_ref, s32[1,8]{1,0:T(1,128)S(1)} %copy-done.3, bf16[768,512]{1,0:T(8,128)(2,1)S(1)} %get-tuple-element.21.mine_ref, bf16[768,512]{1,0:T(8,128)(2,1)S(1)} %collective-permute-done.2.theirs_ref, ...), custom_call_target="tpu_custom_call" | custom-call | flops 7516192768 | bytes 12582912 | tf_op jit(solution)/shard_map/layer/pallas_call | solution.py:303
  94.6 0.4 collective-permute-start.3
  95.0 1.7 %keep.1.half_hbm = bf16[1024,512]{1,0:T(8,128)(2,1)} custom-call(s32[1]{0:T(128)} %bitcast.target_ref.place_ref, bf16[512,1024]{1,0:T(8,128)(2,1)S(1)} %get-tuple-element.26.hidden_ref, bf16[768,512]{1,0:T(8,128)(2,1)S(1)} %get-tuple-element.21.mine_ref, bf16[512,1024]{1,0:T(8,128)(2,1)S(1)} %copy-done, bf16[512,1024]{1,0:T(8,128)(2,1)S(1)} %collective-permute-done.1.wo1_hbm), custom_call_target="tpu_custom_call" | custom-call | flops 536870912 | bytes 3145728 | tf_op jit(solution)/shard_map/keep/pallas_call | solution.py:354
  96.6 0.0 collective-permute-done.3.got_ref
  96.6 0.8 join.1
  (2 shorter events, 0.0 us)
Async XLA Ops:
  0.0 30.2 %collective-permute-start = (bf16[1024,2048]{1,0:T(8,128)(2,1)}, bf16[1024,2048]{1,0:T(8,128)(2,1)}, u32[]{:S(2)}, u32[]{:S(2)}) collective-permute-start(bf16[1024,2048]{1,0:T(8,128)(2,1)} %wq0_ref.1), channel_id=1, source_target_pairs={{0,1},{1,0},{2,3},{3,2},{4,5},{5,4},{6,7},{7,6},{8,9},{9,8},{10,11... | collective-permute-start | bytes 12582920 | tf_op jit(solution)/shard_map/ppermute | solution.py:402
  3.2 27.0 %collective-permute-start.1 = (bf16[512,1024]{1,0:T(8,128)(2,1)}, bf16[512,1024]{1,0:T(8,128)(2,1)S(1)}, u32[]{:S(2)}, u32[]{:S(2)}) collective-permute-start(bf16[512,1024]{1,0:T(8,128)(2,1)} %wo0_hbm.3), channel_id=1, source_target_pairs={{0,1},{1,0},{2,3},{3,2},{4,5},{5,4},{6,7},{7,6},{8,9},{9,8},{10,11... | collective-permute-start | bytes 3145736 | tf_op jit(solution)/shard_map/ppermute | solution.py:403
  5.1 69.0 %copy-start.1 = (s32[8,128]{1,0:T(8,128)S(1)}, s32[8,128]{1,0:T(8,128)}, u32[]{:S(2)}) copy-start(s32[8,128]{1,0:T(8,128)} %get-tuple-element.16) | copy-start | bytes 12292
  34.9 39.2 %all-to-all-start.1 = ((bf16[128,40,128]{2,1,0:T(8,128)(2,1)}), bf16[128,40,128]{2,1,0:T(8,128)(2,1)S(1)}, u32[]{:S(2)}, u32[]{:S(2)}) async-start(bf16[128,40,128]{2,1,0:T(8,128)(2,1)} %bitcast.14), calls=%async_computation.1 | async-start | bytes 2621440 | tf_op jit(solution)/shard_map/all_to_all | solution.py:408
  74.1 8.6 %copy-start = (bf16[512,1024]{1,0:T(8,128)(2,1)S(1)}, bf16[512,1024]{1,0:T(8,128)(2,1)}, u32[]{:S(2)}) copy-start(bf16[512,1024]{1,0:T(8,128)(2,1)} %wo0_hbm.3) | copy-start | bytes 3145732
  74.1 8.6 %copy-start.2 = (bf16[1024,2048]{1,0:T(8,128)(2,1)S(1)}, bf16[1024,2048]{1,0:T(8,128)(2,1)}, u32[]{:S(2)}) copy-start(bf16[1024,2048]{1,0:T(8,128)(2,1)} %wq0_ref.1) | copy-start | bytes 12582916
  74.1 8.7 %copy-start.3 = (s32[1,8]{1,0:T(1,128)S(1)}, s32[1,8]{1,0:T(1,128)}, u32[]{:S(2)}) copy-start(s32[1,8]{1,0:T(1,128)} %lengths_ref.1) | copy-start | bytes 100
  76.1 6.6 %collective-permute-start.2 = (bf16[768,512]{1,0:T(8,128)(2,1)S(1)}, bf16[768,512]{1,0:T(8,128)(2,1)S(1)}, u32[]{:S(2)}, u32[]{:S(2)}) collective-permute-start(bf16[768,512]{1,0:T(8,128)(2,1)S(1)} %get-tuple-element.22), channel_id=1, source_target_pairs={{0,1},{1,0},{2,3},{3,2},{4,5},{5,4},{6,7},{7,6},{8,9},{9,8},{10,11... | collective-permute-start | bytes 2359304 | tf_op jit(solution)/shard_map/ppermute | solution.py:411
  94.6 2.0 %collective-permute-start.3 = (bf16[512,512]{1,0:T(8,128)(2,1)S(1)}, bf16[512,512]{1,0:T(8,128)(2,1)S(1)}, u32[]{:S(2)}, u32[]{:S(2)}) collective-permute-start(bf16[512,512]{1,0:T(8,128)(2,1)S(1)} %get-tuple-element.25), channel_id=1, source_target_pairs={{0,1},{1,0},{2,3},{3,2},{4,5},{5,4},{6,7},{7,6},{8,9},{9,8},{10,11... | collective-permute-start | bytes 1572872 | tf_op jit(solution)/shard_map/ppermute | solution.py:414
